TPU v7x, 32 devices: a whole 2x2x4 slice. The times are simulated.
32 devices in a mesh: fsdp: 16 (over z, x, core), rep: 2 (over y).
Axes of the slice: x: 2, y: 2, z: 4, core: 2. Of those that a mesh axis runs over, the one named last changes fastest.
Arguments:
- tokens: bfloat16 [65536, 768], P(('fsdp', 'rep')), may hold values from -6 to 6
- piece_start: int32 [64, 2], P(('fsdp', 'rep')), may hold values from 1 to 960, as said below
- piece_length: int32 [64, 2], P(('fsdp', 'rep')), may hold values from 64 to 256, as said below
- query_key_value: bfloat16 [768, 2304], P('fsdp'), as said below
- output_weight: bfloat16 [768, 768], P('fsdp'), may hold values from -0.4375 to 0.4375
- up_weight: bfloat16 [768, 3072], P('fsdp'), may hold values from -0.21875 to 0.21875
- down_weight: bfloat16 [3072, 768], P('fsdp'), may hold values from -0.109375 to 0.109375
- first_gain: bfloat16 [768], P('fsdp'), may hold values from 0.099609375 to 1.8984375
- first_shift: bfloat16 [768], P('fsdp'), may hold values from -3 to 3
- second_gain: bfloat16 [768], P('fsdp'), may hold values from 0.099609375 to 1.8984375
- second_shift: bfloat16 [768], P('fsdp'), may hold values from -3 to 3
- up_bias: bfloat16 [3072], P('fsdp'), may hold values from -3 to 3
- down_bias: bfloat16 [768], P('fsdp'), may hold values from -3 to 3
- cotangent: bfloat16 [65536, 768], P(('fsdp', 'rep')), may hold values from -6 to 6
Outputs:
- block_output: bfloat16 [65536, 768], P(('fsdp', 'rep'))
- grad_tokens: float32 [65536, 768], P(('fsdp', 'rep'))
- grad_query_key_value: float32 [768, 2304], P('fsdp')
- grad_output_weight: float32 [768, 768], P('fsdp')
- grad_up_weight: float32 [768, 3072], P('fsdp')
- grad_down_weight: float32 [3072, 768], P('fsdp')
- grad_first_gain: float32 [768], P('fsdp')
- grad_first_shift: float32 [768], P('fsdp')
- grad_second_gain: float32 [768], P('fsdp')
- grad_second_shift: float32 [768], P('fsdp')
- grad_up_bias: float32 [3072], P('fsdp')
- grad_down_bias: float32 [768], P('fsdp')
Inputs may be any that keep to these rules, and one draw needn't show every extreme that they name: `piece_start`: piece p of a sequence starts in positions p * 512 + 1 to (p + 1) * 512 - 1 and ends before (p + 1) * 512; pieces never intersect and never hold position 0. `piece_length`: the first piece of every sequence has exactly 256 tokens. `query_key_value`: entries have a deviation of about 1 / sqrt(768) and lie within four such deviations; columns 0 to 64 - 1 (head 0's queries) are a hundred times smaller.
All inputs are finite; a program needn't handle non-finite values.
Results may differ from a plain program's by a relative error of at most 0.023.
The roundings to bfloat16 on the way count: a program that leaves them out, or rounds other values in their place, can miss the bound.
Values may be sent and summed in bfloat16 or wider, within the bound.
A program may use at most 512 MiB of HBM per device.

v0:
```python
import jax
import jax.numpy as jnp
from jax import lax
from jax.sharding import PartitionSpec as P

HEAD_DIM = 64
QB = 512


MASKED_VALUE = -1e30
EPSILON = 1e-05


def as_sent(value):
    return jax.tree.map(lambda a: a.astype(jnp.bfloat16) if a.dtype == jnp.float32 else a, value)


def layer_norm(values, gain, shift):
    center = values - jnp.mean(values, axis=-1, keepdims=True)
    spread = jnp.mean(center * center, axis=-1, keepdims=True)
    return center * lax.rsqrt(spread + EPSILON) * gain + shift


def gelu_tanh(values):
    return jax.nn.gelu(values, approximate=True)


def piece_labels(starts, lengths, length):
    positions = jnp.arange(length, dtype=jnp.int32)
    inside = (positions[:, None] >= starts[None, :]) & (
        positions[:, None] < starts[None, :] + lengths[None, :]
    )
    numbers = jnp.arange(1, starts.shape[0] + 1, dtype=jnp.int32)
    return jnp.sum(jnp.where(inside, numbers[None, :], 0), axis=1)


def masked_rowsum(triangle, values):
    upper_part = values.astype(jnp.bfloat16)
    remainder = values - upper_part.astype(jnp.float32)
    middle_part = remainder.astype(jnp.bfloat16)
    lower_part = (remainder - middle_part.astype(jnp.float32)).astype(jnp.bfloat16)
    total = jnp.dot(triangle, upper_part, preferred_element_type=jnp.float32)
    total = total + jnp.dot(triangle, middle_part, preferred_element_type=jnp.float32)
    return total + jnp.dot(triangle, lower_part, preferred_element_type=jnp.float32)


def block_masks(labels, first_row, row_count):
    length = labels.shape[0]
    query_pos = first_row + jnp.arange(row_count, dtype=jnp.int32)
    key_pos = jnp.arange(length, dtype=jnp.int32)
    query_labels = labels[first_row : first_row + row_count]
    allowed = (key_pos[None, :] <= query_pos[:, None]) | (
        query_labels[:, None] == labels[None, :]
    ) & (query_labels[:, None] > 0)
    chosen_mask = allowed & (key_pos[None, :] != 0) & (key_pos[None, :] != query_pos[:, None])
    return (allowed, chosen_mask)


def block_logits(query_block, key_rows, allowed, chosen_mask, strict_lower, prefix):
    factor = HEAD_DIM ** (-0.5)
    scores = (
        jnp.einsum("qhd,khd->hqk", query_block, key_rows, preferred_element_type=jnp.float32)
        * factor
    )
    selected = jnp.where(chosen_mask & (scores[0] > 0), scores[0], 0.0)
    penalty = prefix[None, :] + masked_rowsum(strict_lower, selected)
    logits = jnp.where(allowed[None], scores - penalty[None], MASKED_VALUE)
    return (scores, selected, logits)


def split_heads(projected):
    length = projected.shape[0]
    head_count = projected.shape[1] // (3 * HEAD_DIM)
    split_parts = projected.reshape(length, 3, head_count, HEAD_DIM)
    return (split_parts[:, 0], split_parts[:, 1], split_parts[:, 2])


def attend(projected, labels, strict_lower):
    queries, key_rows, value_rows = split_heads(projected)
    length = projected.shape[0]
    block_rows = strict_lower.shape[0]
    prefix = jnp.zeros((length,), jnp.float32)
    pieces, totals, prefixes = ([], [], [])
    for block_id in range(length // block_rows):
        first_row = block_id * block_rows
        allowed, chosen_mask = block_masks(labels, first_row, block_rows)
        query_block = queries[first_row : first_row + block_rows]
        scores, selected, logits = block_logits(
            query_block, key_rows, allowed, chosen_mask, strict_lower, prefix
        )
        prefixes.append(prefix)
        prefix = prefix + jnp.sum(selected, axis=0)
        largest = jnp.max(logits, axis=-1, keepdims=True)
        log_total = largest + jnp.log(jnp.sum(jnp.exp(logits - largest), axis=-1, keepdims=True))
        attention = jnp.exp(logits - log_total).astype(jnp.bfloat16)
        pieces.append(
            jnp.einsum("hqk,khd->qhd", attention, value_rows, preferred_element_type=jnp.float32)
        )
        totals.append(log_total)
    mixed_rows = jnp.concatenate(pieces, axis=0).reshape(length, -1).astype(jnp.bfloat16)
    return (mixed_rows, totals, prefixes)


def attend_back(projected, labels, grad_mixed, totals, prefixes, strict_lower):
    queries, key_rows, value_rows = split_heads(projected)
    length = projected.shape[0]
    block_rows = strict_lower.shape[0]
    factor = HEAD_DIM ** (-0.5)
    strict_upper = strict_lower.T
    grad_heads = grad_mixed.reshape(length, -1, HEAD_DIM)
    grad_keys = jnp.zeros(key_rows.shape, jnp.float32)
    grad_values = jnp.zeros(value_rows.shape, jnp.float32)
    later_sum = jnp.zeros((length,), jnp.float32)
    grad_queries = []
    for block_id in reversed(range(length // block_rows)):
        first_row = block_id * block_rows
        allowed, chosen_mask = block_masks(labels, first_row, block_rows)
        query_block = queries[first_row : first_row + block_rows]
        scores, selected, logits = block_logits(
            query_block, key_rows, allowed, chosen_mask, strict_lower, prefixes[block_id]
        )
        attention = jnp.exp(logits - totals[block_id])
        grad_block = grad_heads[first_row : first_row + block_rows]
        grad_attention = jnp.einsum(
            "qhd,khd->hqk", grad_block, value_rows, preferred_element_type=jnp.float32
        )
        inner_sum = jnp.sum(grad_attention * attention, axis=-1, keepdims=True)
        grad_logits = attention * (grad_attention - inner_sum)
        grad_penalty = -jnp.sum(grad_logits, axis=0)
        grad_selected = later_sum[None, :] + masked_rowsum(strict_upper, grad_penalty)
        later_sum = later_sum + jnp.sum(grad_penalty, axis=0)
        grad_first = grad_logits[0] + jnp.where(chosen_mask & (scores[0] > 0), grad_selected, 0.0)
        grad_scores = jnp.concatenate([grad_first[None], grad_logits[1:]], axis=0).astype(
            jnp.bfloat16
        )
        grad_queries.append(
            jnp.einsum("hqk,khd->qhd", grad_scores, key_rows, preferred_element_type=jnp.float32)
            * factor
        )
        grad_keys = (
            grad_keys
            + jnp.einsum(
                "hqk,qhd->khd", grad_scores, query_block, preferred_element_type=jnp.float32
            )
            * factor
        )
        grad_values = grad_values + jnp.einsum(
            "hqk,qhd->khd",
            attention.astype(jnp.bfloat16),
            grad_block,
            preferred_element_type=jnp.float32,
        )
    grad_query_rows = jnp.concatenate(grad_queries[::-1], axis=0)
    stacked = jnp.stack([grad_query_rows, grad_keys, grad_values], axis=1)
    return stacked.reshape(length, -1).astype(jnp.bfloat16)


def forward_pass(rows_in, starts, lengths, weights, strict_lower):
    (
        query_key_value,
        output_weight,
        up_weight,
        down_weight,
        first_gain,
        first_shift,
        second_gain,
        second_shift,
        up_bias,
        down_bias,
    ) = weights
    rows_wide = rows_in.astype(jnp.float32)
    normed_first = layer_norm(
        rows_wide, first_gain.astype(jnp.float32), first_shift.astype(jnp.float32)
    ).astype(jnp.bfloat16)
    projected = jnp.dot(normed_first, query_key_value, preferred_element_type=jnp.float32).astype(
        jnp.bfloat16
    )
    labels = piece_labels(starts, lengths, rows_in.shape[0])
    mixed_rows, totals, prefixes = attend(projected, labels, strict_lower)
    middle = rows_wide + jnp.dot(mixed_rows, output_weight, preferred_element_type=jnp.float32)
    normed_second = layer_norm(
        middle, second_gain.astype(jnp.float32), second_shift.astype(jnp.float32)
    ).astype(jnp.bfloat16)
    before_act = jnp.dot(
        normed_second, up_weight, preferred_element_type=jnp.float32
    ) + up_bias.astype(jnp.float32)
    hidden = gelu_tanh(before_act).astype(jnp.bfloat16)
    result = middle + (
        jnp.dot(hidden, down_weight, preferred_element_type=jnp.float32)
        + down_bias.astype(jnp.float32)
    )
    kept = (
        normed_first,
        projected,
        labels,
        mixed_rows,
        totals,
        prefixes,
        middle,
        normed_second,
        before_act,
        hidden,
    )
    return (result.astype(jnp.bfloat16), kept)


def backward_pass(rows_in, grad_rows, kept, weights, strict_lower):
    (
        query_key_value,
        output_weight,
        up_weight,
        down_weight,
        first_gain,
        first_shift,
        second_gain,
        second_shift,
        up_bias,
        down_bias,
    ) = weights
    (
        normed_first,
        projected,
        labels,
        mixed_rows,
        totals,
        prefixes,
        middle,
        normed_second,
        before_act,
        hidden,
    ) = kept
    grad_out = grad_rows.astype(jnp.float32)
    grad_branch = grad_out.astype(jnp.bfloat16)
    grad_down_bias = jnp.sum(grad_branch.astype(jnp.float32), axis=0)
    grad_down_weight = jnp.einsum(
        "tf,td->fd", hidden, grad_branch, preferred_element_type=jnp.float32
    )
    grad_hidden = jnp.einsum(
        "td,fd->tf", grad_branch, down_weight, preferred_element_type=jnp.float32
    ).astype(jnp.bfloat16)
    _, gelu_pull = jax.vjp(gelu_tanh, before_act)
    grad_before = gelu_pull(grad_hidden.astype(jnp.float32))[0].astype(jnp.bfloat16)
    grad_up_bias = jnp.sum(grad_before.astype(jnp.float32), axis=0)
    grad_up_weight = jnp.einsum(
        "td,tf->df", normed_second, grad_before, preferred_element_type=jnp.float32
    )
    grad_normed_second = jnp.einsum(
        "tf,df->td", grad_before, up_weight, preferred_element_type=jnp.float32
    )
    _, second_pull = jax.vjp(
        layer_norm, middle, second_gain.astype(jnp.float32), second_shift.astype(jnp.float32)
    )
    grad_middle_norm, grad_second_gain, grad_second_shift = second_pull(grad_normed_second)
    grad_middle = grad_out + grad_middle_norm
    grad_proj = grad_middle.astype(jnp.bfloat16)
    grad_output_weight = jnp.einsum(
        "tc,td->cd", mixed_rows, grad_proj, preferred_element_type=jnp.float32
    )
    grad_mixed = jnp.einsum(
        "td,cd->tc", grad_proj, output_weight, preferred_element_type=jnp.float32
    ).astype(jnp.bfloat16)
    grad_projected = attend_back(projected, labels, grad_mixed, totals, prefixes, strict_lower)
    grad_query_key_value = jnp.einsum(
        "td,te->de", normed_first, grad_projected, preferred_element_type=jnp.float32
    )
    grad_normed_first = jnp.einsum(
        "te,de->td", grad_projected, query_key_value, preferred_element_type=jnp.float32
    )
    _, first_pull = jax.vjp(
        layer_norm,
        rows_in.astype(jnp.float32),
        first_gain.astype(jnp.float32),
        first_shift.astype(jnp.float32),
    )
    grad_input_norm, grad_first_gain, grad_first_shift = first_pull(grad_normed_first)
    grad_input = grad_middle + grad_input_norm
    grads = (
        grad_query_key_value,
        grad_output_weight,
        grad_up_weight,
        grad_down_weight,
        grad_first_gain,
        grad_first_shift,
        grad_second_gain,
        grad_second_shift,
        grad_up_bias,
        grad_down_bias,
    )
    return (grad_input, grads)


def run_batches(
    tokens, piece_start, piece_length, cotangent, fetch_forward, fetch_backward, strict_lower
):
    batches = piece_start.shape[0]
    seq_rows = tokens.shape[0] // batches
    outputs, input_grads = ([], [])
    owned_grads = None
    summed_grads = None
    for batch_id in range(batches):
        first_row = batch_id * seq_rows
        rows_in = tokens[first_row : first_row + seq_rows]
        grad_rows = cotangent[first_row : first_row + seq_rows]
        weights = fetch_forward()
        result, kept = forward_pass(
            rows_in, piece_start[batch_id], piece_length[batch_id], weights, strict_lower
        )
        grad_input, grads = backward_pass(
            rows_in, grad_rows, kept, fetch_backward(weights), strict_lower
        )
        outputs.append(result)
        input_grads.append(grad_input)
        summed_grads = (
            grads
            if summed_grads is None
            else tuple((left + right for left, right in zip(summed_grads, grads)))
        )
    owned_grads = jax.tree.map(
        lambda part: part.astype(jnp.float32),
        lax.psum_scatter(as_sent(summed_grads), "fsdp", scatter_dimension=0, tiled=True),
    )
    return (jnp.concatenate(outputs, axis=0), jnp.concatenate(input_grads, axis=0), owned_grads)


def local(
    tokens,
    piece_start,
    piece_length,
    query_key_value,
    output_weight,
    up_weight,
    down_weight,
    first_gain,
    first_shift,
    second_gain,
    second_shift,
    up_bias,
    down_bias,
    cotangent,
):
    params = (
        query_key_value,
        output_weight,
        up_weight,
        down_weight,
        first_gain,
        first_shift,
        second_gain,
        second_shift,
        up_bias,
        down_bias,
    )
    row_index = lax.broadcasted_iota(jnp.int32, (QB, QB), 0)
    col_index = lax.broadcasted_iota(jnp.int32, (QB, QB), 1)
    strict_lower = (col_index < row_index).astype(jnp.bfloat16)

    def fetch_forward():
        return (
            lax.all_gather(params[0], "fsdp", axis=0, tiled=True),
            lax.all_gather(params[1], "fsdp", axis=0, tiled=True),
            lax.all_gather(params[2], "fsdp", axis=0, tiled=True),
            lax.all_gather(params[3], "fsdp", axis=0, tiled=True),
            lax.all_gather(params[4], "fsdp", axis=0, tiled=True),
            lax.all_gather(params[5], "fsdp", axis=0, tiled=True),
            lax.all_gather(params[6], "fsdp", axis=0, tiled=True),
            lax.all_gather(params[7], "fsdp", axis=0, tiled=True),
            lax.all_gather(params[8], "fsdp", axis=0, tiled=True),
            lax.all_gather(params[9], "fsdp", axis=0, tiled=True),
        )

    def fetch_backward(held):
        return (
            lax.all_gather(params[0], "fsdp", axis=0, tiled=True),
            lax.all_gather(params[1], "fsdp", axis=0, tiled=True),
            lax.all_gather(params[2], "fsdp", axis=0, tiled=True),
            lax.all_gather(params[3], "fsdp", axis=0, tiled=True),
            lax.all_gather(params[4], "fsdp", axis=0, tiled=True),
            lax.all_gather(params[5], "fsdp", axis=0, tiled=True),
            lax.all_gather(params[6], "fsdp", axis=0, tiled=True),
            lax.all_gather(params[7], "fsdp", axis=0, tiled=True),
            lax.all_gather(params[8], "fsdp", axis=0, tiled=True),
            lax.all_gather(params[9], "fsdp", axis=0, tiled=True),
        )

    block_output, grad_tokens, owned_grads = run_batches(
        tokens, piece_start, piece_length, cotangent, fetch_forward, fetch_backward, strict_lower
    )
    totals = jax.tree.map(
        lambda part: part.astype(jnp.float32), lax.psum(as_sent(owned_grads), "rep")
    )
    return (
        block_output,
        grad_tokens,
        totals[0],
        totals[1],
        totals[2],
        totals[3],
        totals[4],
        totals[5],
        totals[6],
        totals[7],
        totals[8],
        totals[9],
    )


def solution(mesh):
    placed = (
        P(("fsdp", "rep"), None),
        P(("fsdp", "rep"), None),
        P(("fsdp", "rep"), None),
        P("fsdp", None),
        P("fsdp", None),
        P("fsdp", None),
        P("fsdp", None),
        P("fsdp"),
        P("fsdp"),
        P("fsdp"),
        P("fsdp"),
        P("fsdp"),
        P("fsdp"),
        P(("fsdp", "rep"), None),
    )
    return jax.shard_map(
        local,
        mesh=mesh,
        in_specs=placed,
        out_specs=(
            P(("fsdp", "rep"), None),
            P(("fsdp", "rep"), None),
            P("fsdp", None),
            P("fsdp", None),
            P("fsdp", None),
            P("fsdp", None),
            P("fsdp"),
            P("fsdp"),
            P("fsdp"),
            P("fsdp"),
            P("fsdp"),
            P("fsdp"),
        ),
        check_vma=False,
    )
```

profile of v0, /device:TPU:0, one launch (start us, length us, event | category | flops | bytes accessed | tf_op | source)
XLA Modules:
  0.0 1133.3 jit_solution(1819834134296805344)
XLA Ops:
  17.8 63.6 %all-reduce.13 = (bf16[768]{0:T(1024)(128)(2,1)S(1)}, bf16[768]{0:T(1024)(128)(2,1)S(1)}, bf16[768]{0:T(1024)(128)(2,1)S(1)}, bf16[768]{0:T(1024)(128)(2,1)S(1)}, bf16[3072]{0:T(1024)(128)(2,1)S(1)}) all-reduce(bf16[768]{0:T(1024)(128)(2,1)S(1)} %dynamic-update-slice.1, ...), channel_id=1, replica_groups=mesh['fsdp'=16,'rep'=2] {'fsdp'}, use_global_device_ids=true, to_apply=%add.1 | all-reduce | flops 6144 | bytes 24576
  99.3 7.8 convolution_convert_fusion.1
  113.7 13.6 %broadcast_multiply_fusion.2 = f32[12,512,1024]{2,1,0:T(8,128)} fusion(bf16[1024,3,12,64]{0,3,2,1:T(8,128)(2,1)} %bitcast.291), kind=kOutput, calls=%fused_computation.70 | convolution fusion | flops 811597824 | bytes 27525120 | tf_op jit(solution)/shard_map/qhd,khd->hqk/dot_general | solution.py:62
  127.4 10.3 broadcast_multiply_fusion.3
  155.5 8.0 fusion.68
  203.6 13.0 %fusion.3 = f32[12,512]{1,0:T(8,128)S(1)} fusion(f32[12,512,1024]{2,1,0:T(8,128)} %copy-done.1, f32[512,1024]{1,0:T(8,128)S(1)} %add_add_fusion.6, pred[512,1024]{1,0:T(8,128)(4,1)S(1)} %copy-done.41), kind=kLoop, calls=%fused_computation.27 | loop fusion | flops 18868224 | bytes 27811840 | tf_op jit(solution)/shard_map/reduce_max | solution.py:93
  216.8 9.5 exponential_reduce_fusion
  230.3 12.9 %fusion.1 = f32[12,512]{1,0:T(8,128)S(1)} fusion(f32[12,512,1024]{2,1,0:T(8,128)} %broadcast_multiply_fusion.2, f32[512,1024]{1,0:T(8,128)S(1)} %add_add_fusion.8, pred[512,1024]{1,0:T(8,128)(4,1)S(1)} %copy-done.44), kind=kLoop, calls=%fused_computation.25 | loop fusion | flops 18868224 | bytes 27811840 | tf_op jit(solution)/shard_map/reduce_max | solution.py:93
  250.6 13.3 %fusion.113 = bf16[512,12,64]{0,2,1:T(8,128)(2,1)} fusion(bf16[1024,3,12,64]{0,3,2,1:T(8,128)(2,1)} %bitcast.292, f32[12,512,1024]{2,1,0:T(8,128)} %broadcast_multiply_fusion.2, f32[12,512]{1,0:T(8,128)S(1)} %log_add_fusion.2, f32[512,1024]{1,0:T(8,128)} %copy-done.8, pred[512,1024]{1,0:T(8,128)(4,1)} %get-tuple-element.145), kind=kOutput, calls=%fused_computation.249 | convolution fusion | flops 830865408 | bytes 30171136 | tf_op jit(solution)/shard_map/hqk,khd->qhd/dot_general | solution.py:97
  267.0 11.5 %fusion = f32[12,512]{1,0:T(8,128)S(1)} fusion(f32[12,512,1024]{2,1,0:T(8,128)} %broadcast_multiply_fusion.3, f32[512,1024]{1,0:T(8,128)S(1)} %add_add_fusion.9, pred[512,1024]{1,0:T(8,128)(4,1)S(1)} %get-tuple-element.143), kind=kLoop, calls=%fused_computation.24 | loop fusion | flops 18868224 | bytes 27811840 | tf_op jit(solution)/shard_map/reduce_max | solution.py:93
  278.5 11.8 %exponential_reduce_fusion.3 = f32[12,512]{1,0:T(8,128)S(1)} fusion(f32[12,512,1024]{2,1,0:T(8,128)} %broadcast_multiply_fusion.3, f32[12,512]{1,0:T(8,128)S(1)} %fusion, f32[512,1024]{1,0:T(8,128)S(1)} %add_add_fusion.9, pred[512,1024]{1,0:T(8,128)(4,1)S(1)} %get-tuple-element.143), kind=kLoop, calls=%fused_computation.18 | loop fusion | flops 25159680 | bytes 27836416 | tf_op jit(solution)/shard_map/reduce_sum | solution.py:94
  290.4 12.6 %fusion.112 = bf16[512,12,64]{0,2,1:T(8,128)(2,1)} fusion(bf16[1024,3,12,64]{0,3,2,1:T(8,128)(2,1)} %bitcast.293, f32[12,512,1024]{2,1,0:T(8,128)} %broadcast_multiply_fusion.3, f32[12,512]{1,0:T(8,128)S(1)} %log_add_fusion.3, f32[512,1024]{1,0:T(8,128)S(1)} %add_add_fusion.9, pred[512,1024]{1,0:T(8,128)(4,1)S(1)} %get-tuple-element.143), kind=kOutput, calls=%fused_computation.248 | convolution fusion | flops 830865408 | bytes 30171136 | tf_op jit(solution)/shard_map/hqk,khd->qhd/dot_general | solution.py:97
  306.7 12.0 %fusion.2 = f32[12,512]{1,0:T(8,128)S(1)} fusion(f32[12,512,1024]{2,1,0:T(8,128)} %copy-done, f32[512,1024]{1,0:T(8,128)S(1)} %add_add_fusion.7, pred[512,1024]{1,0:T(8,128)(4,1)S(1)} %copy-done.39), kind=kLoop, calls=%fused_computation.26 | loop fusion | flops 18868224 | bytes 27811840 | tf_op jit(solution)/shard_map/reduce_max | solution.py:93
  318.7 12.1 %exponential_reduce_fusion.1 = f32[12,512]{1,0:T(8,128)S(1)} fusion(f32[12,512,1024]{2,1,0:T(8,128)} %copy-done, f32[12,512]{1,0:T(8,128)S(1)} %fusion.2, f32[512,1024]{1,0:T(8,128)S(1)} %add_add_fusion.7, pred[512,1024]{1,0:T(8,128)(4,1)S(1)} %copy-done.39), kind=kLoop, calls=%fused_computation.12 | loop fusion | flops 25159680 | bytes 27836416 | tf_op jit(solution)/shard_map/reduce_sum | solution.py:94
  332.3 13.0 %fusion.115 = bf16[512,12,64]{0,2,1:T(8,128)(2,1)} fusion(bf16[1024,3,12,64]{0,3,2,1:T(8,128)(2,1)} %bitcast.279, f32[12,512,1024]{2,1,0:T(8,128)} %copy-done.1, f32[12,512]{1,0:T(8,128)S(1)} %log_add_fusion, f32[512,1024]{1,0:T(8,128)} %copy-done.6, pred[512,1024]{1,0:T(8,128)(4,1)S(1)} %copy-done.42), kind=kOutput, calls=%fused_computation.251 | convolution fusion | flops 830865408 | bytes 30171136 | tf_op jit(solution)/shard_map/hqk,khd->qhd/dot_general | solution.py:97
  345.3 12.9 %fusion.114 = bf16[512,12,64]{0,2,1:T(8,128)(2,1)} fusion(bf16[1024,3,12,64]{0,3,2,1:T(8,128)(2,1)} %bitcast.280, f32[12,512,1024]{2,1,0:T(8,128)} %copy-done, f32[12,512]{1,0:T(8,128)S(1)} %log_add_fusion.1, f32[512,1024]{1,0:T(8,128)S(1)} %add_add_fusion.7, pred[512,1024]{1,0:T(8,128)(4,1)S(1)} %copy-done.39), kind=kOutput, calls=%fused_computation.250 | convolution fusion | flops 830865408 | bytes 30171136 | tf_op jit(solution)/shard_map/hqk,khd->qhd/dot_general | solution.py:97
  371.3 11.1 fusion.203
  382.4 17.1 %convert_reduce_fusion.1 = (f32[3072]{0:T(1024)}, bf16[1024,3072]{1,0:T(8,128)(2,1)S(1)}) fusion(f32[1024,3072]{1,0:T(8,128)} %fusion.203, f32[3072]{0:T(1024)S(1)} %copy-done.130, bf16[3072,768]{1,0:T(8,128)(2,1)} %all-gather.11.cloned.1.call-done, bf16[2048,768]{1,0:T(8,128)(2,1)} %param.27), kind=kOutput, calls=%fused_computation.65 | convolution fusion | flops 4910478336 | bytes 25190400 | tf_op jit(solution)/shard_map/td,fd->tf/dot_general | solution.py:238
  410.4 11.4 %fusion.204 = f32[1024,3072]{1,0:T(8,128)} fusion(bf16[768,3072]{1,0:T(8,128)(2,1)} %all-gather.9.cloned.1.call-done, f32[1024,768]{0,1:T(8,128)} %copy-done.22, f32[1024]{0:T(1024)S(1)} %fusion.157, f32[1024]{0:T(1024)S(1)} %broadcast_multiply_fusion.4, f32[768]{0:T(1024)S(1)} %copy-done.85, f32[768]{0:T(1024)S(1)} %copy-done.83), kind=kOutput, calls=%fused_computation.352 | convolution fusion | flops 4835770368 | bytes 20461568 | tf_op jit(solution)/shard_map/dot_general | solution.py:184
  421.8 15.6 %convert_reduce_fusion = (f32[3072]{0:T(1024)}, bf16[1024,3072]{1,0:T(8,128)(2,1)S(1)}) fusion(f32[1024,3072]{1,0:T(8,128)} %fusion.204, f32[3072]{0:T(1024)S(1)} %copy-done.130, bf16[3072,768]{1,0:T(8,128)(2,1)} %all-gather.11.cloned.1.call-done, bf16[2048,768]{1,0:T(8,128)(2,1)S(1)} %copy-done.76), kind=kOutput, calls=%fused_computation.64 | convolution fusion | flops 4910478336 | bytes 25190400 | tf_op jit(solution)/shard_map/td,fd->tf/dot_general | solution.py:238
  467.4 21.7 %multiply_reduce_fusion.3 = (f32[12,512]{1,0:T(8,128)S(1)}, f32[12,512,1024]{2,1,0:T(8,128)}) fusion(f32[12,512,1024]{2,1,0:T(8,128)} %broadcast_multiply_fusion.3, f32[12,512]{1,0:T(8,128)S(1)} %log_add_fusion.3, f32[512,1024]{1,0:T(8,128)S(1)} %add_add_fusion.9, pred[512,1024]{1,0:T(8,128)(4,1)S(1)} %get-tuple-element.143, ...), kind=kOutput, calls=%fused_computation.7 | convolution fusion | flops 836757504 | bytes 55369728 | tf_op jit(solution)/shard_map/qhd,khd->hqk/dot_general | solution.py:124
  489.1 25.0 %fusion.209 = (f32[512,1024]{1,0:T(8,128)S(1)}, f32[12,512,1024]{2,1,0:T(8,128)}) fusion(f32[12,512,1024]{2,1,0:T(8,128)} %get-tuple-element.161, f32[12,512]{1,0:T(8,128)S(1)} %get-tuple-element.160, f32[12,512]{1,0:T(8,128)S(1)} %log_add_fusion.3, f32[12,512,1024]{2,1,0:T(8,128)} %broadcast_multiply_fusion.3, f32[512,1024]{1,0:T(8,128)S(1)} %add_add_fusion.9, ...), kind=kLoop, calls=%fused_computation.357 | loop fusion | flops 37224448 | bytes 80265216 | tf_op jit(solution)/shard_map/reduce_sum | solution.py:129
  518.2 13.2 %fusion.199 = f32[12,64,1024]{2,1,0:T(8,128)} fusion(bf16[512,12,64]{0,2,1:T(8,128)(2,1)S(1)} %bitcast.313, f32[12,512,1024]{2,1,0:T(8,128)} %broadcast_multiply_fusion.2, f32[12,512]{1,0:T(8,128)S(1)} %copy-done.104, f32[512,1024]{1,0:T(8,128)S(1)} %copy-done.9, pred[512,1024]{1,0:T(8,128)(4,1)S(1)} %copy-done.45), kind=kOutput, calls=%fused_computation.349 | convolution fusion | flops 830472192 | bytes 31744000 | tf_op jit(solution)/shard_map/hqk,qhd->khd/dot_general | solution.py:147
  531.4 21.6 %multiply_reduce_fusion.2 = (f32[12,512]{1,0:T(8,128)S(1)}, f32[12,512,1024]{2,1,0:T(8,128)}) fusion(f32[12,512,1024]{2,1,0:T(8,128)} %broadcast_multiply_fusion.2, f32[12,512]{1,0:T(8,128)S(1)} %copy-done.104, f32[512,1024]{1,0:T(8,128)S(1)} %copy-done.9, pred[512,1024]{1,0:T(8,128)(4,1)S(1)} %copy-done.45, bf16[512,12,64]{0,2,1:T(8,128)(2,1)S(1)} %bitcast.314, ...), kind=kOutput, calls=%fused_computation.5 | convolution fusion | flops 836757504 | bytes 55369728 | tf_op jit(solution)/shard_map/qhd,khd->hqk/dot_general | solution.py:124
  553.0 25.9 %fusion.205 = (f32[1024]{0:T(1024)}, f32[512,1024]{1,0:T(8,128)S(1)}, f32[12,512,1024]{2,1,0:T(8,128)}) fusion(f32[12,512,1024]{2,1,0:T(8,128)} %get-tuple-element.159, f32[12,512]{1,0:T(8,128)S(1)} %get-tuple-element.158, f32[12,512]{1,0:T(8,128)S(1)} %copy-done.104, f32[12,512,1024]{2,1,0:T(8,128)} %broadcast_multiply_fusion.2, ...), kind=kLoop, calls=%fused_computation.353 | loop fusion | flops 43514880 | bytes 80269312 | tf_op jit(solution)/shard_map/reduce_sum | solution.py:131
  580.4 12.6 %slice.406 = bf16[11,512,1024]{2,1,0:T(8,128)(2,1)} slice(f32[12,512,1024]{2,1,0:T(8,128)} %get-tuple-element.104), slice={[1:12], [0:512], [0:1024]} | slice | bytes 23068672 | tf_op jit(solution)/shard_map/slice | solution.py:133
  595.9 7.9 fusion.117
  613.0 22.8 %multiply_reduce_fusion.1 = (f32[12,512]{1,0:T(8,128)S(1)}, f32[12,512,1024]{2,1,0:T(8,128)}) fusion(f32[12,512,1024]{2,1,0:T(8,128)} %copy-done, f32[12,512]{1,0:T(8,128)S(1)} %copy-done.100, f32[512,1024]{1,0:T(8,128)S(1)} %copy-done.5, pred[512,1024]{1,0:T(8,128)(4,1)S(1)} %copy-done.40, bf16[512,12,64]{0,2,1:T(8,128)(2,1)S(1)} %bitcast.311, ...), kind=kOutput, calls=%fused_computation.3 | convolution fusion | flops 836757504 | bytes 55369728 | tf_op jit(solution)/shard_map/qhd,khd->hqk/dot_general | solution.py:124
  635.8 25.1 %fusion.207 = (f32[512,1024]{1,0:T(8,128)S(1)}, f32[12,512,1024]{2,1,0:T(8,128)}) fusion(f32[12,512,1024]{2,1,0:T(8,128)} %get-tuple-element.165, f32[12,512]{1,0:T(8,128)S(1)} %get-tuple-element.164, f32[12,512]{1,0:T(8,128)S(1)} %copy-done.100, f32[12,512,1024]{2,1,0:T(8,128)} %copy-done, f32[512,1024]{1,0:T(8,128)S(1)} %copy-done.5, ...), kind=kLoop, calls=%fused_computation.355 | loop fusion | flops 37224448 | bytes 80265216 | tf_op jit(solution)/shard_map/reduce_sum | solution.py:129
  665.1 13.2 %fusion.196 = f32[12,64,1024]{2,1,0:T(8,128)} fusion(bf16[512,12,64]{0,2,1:T(8,128)(2,1)S(1)} %bitcast.315, f32[12,512,1024]{2,1,0:T(8,128)} %copy-done.1, f32[12,512]{1,0:T(8,128)S(1)} %copy-done.102, f32[512,1024]{1,0:T(8,128)S(1)} %copy-done.7, pred[512,1024]{1,0:T(8,128)(4,1)S(1)} %copy-done.43), kind=kOutput, calls=%fused_computation.348 | convolution fusion | flops 830472192 | bytes 31744000 | tf_op jit(solution)/shard_map/hqk,qhd->khd/dot_general | solution.py:147
  678.3 21.4 %multiply_reduce_fusion = (f32[12,512]{1,0:T(8,128)S(1)}, f32[12,512,1024]{2,1,0:T(8,128)}) fusion(f32[12,512,1024]{2,1,0:T(8,128)} %copy-done.1, f32[12,512]{1,0:T(8,128)S(1)} %copy-done.102, f32[512,1024]{1,0:T(8,128)S(1)} %copy-done.7, pred[512,1024]{1,0:T(8,128)(4,1)S(1)} %copy-done.43, bf16[512,12,64]{0,2,1:T(8,128)(2,1)S(1)} %bitcast.316, ...), kind=kOutput, calls=%fused_computation.1 | convolution fusion | flops 836757504 | bytes 55369728 | tf_op jit(solution)/shard_map/qhd,khd->hqk/dot_general | solution.py:124
  699.7 25.4 %fusion.206 = (f32[1024]{0:T(1024)S(1)}, f32[512,1024]{1,0:T(8,128)S(1)}, f32[12,512,1024]{2,1,0:T(8,128)}) fusion(f32[12,512,1024]{2,1,0:T(8,128)} %get-tuple-element.163, f32[12,512]{1,0:T(8,128)S(1)} %get-tuple-element.162, f32[12,512]{1,0:T(8,128)S(1)} %copy-done.102, f32[12,512,1024]{2,1,0:T(8,128)} %copy-done.1, f32[512,1024]{1,0:T(8,128)S(1)} %copy-done.7, ...), kind=kLoop, calls=%fused_computation.354 | loop fusion | flops 43514880 | bytes 80269312 | tf_op jit(solution)/shard_map/reduce_sum | solution.py:131
  732.8 15.1 %fusion.89 = bf16[1024,1,12,64]{0,3,2,1:T(8,128)(2,1)} fusion(f32[12,64,1024]{2,1,0:T(8,128)} %fusion.196, bf16[512,12,64]{0,2,1:T(8,128)(2,1)} %bitcast.312, f32[12,512,1024]{2,1,0:T(8,128)} %copy-done, f32[12,512]{1,0:T(8,128)S(1)} %copy-done.100, f32[512,1024]{1,0:T(8,128)} %copy-done.4, pred[512,1024]{1,0:T(8,128)(4,1)S(1)} %copy-done.40), kind=kOutput, calls=%fused_computation.223 | convolution fusion | flops 832045056 | bytes 33316864 | tf_op jit(solution)/shard_map/hqk,qhd->khd/dot_general | solution.py:147
  748.0 14.1 %fusion.88 = bf16[1024,1,12,64]{0,3,2,1:T(8,128)(2,1)} fusion(f32[12,64,1024]{2,1,0:T(8,128)} %fusion.199, bf16[512,12,64]{0,2,1:T(8,128)(2,1)S(1)} %bitcast.310, f32[12,512,1024]{2,1,0:T(8,128)} %broadcast_multiply_fusion.3, f32[12,512]{1,0:T(8,128)S(1)} %copy-done.98, f32[512,1024]{1,0:T(8,128)S(1)} %copy-done.3, pred[512,1024]{1,0:T(8,128)(4,1)S(1)} %copy-done.38), kind=kOutput, calls=%fused_computation.222 | convolution fusion | flops 832045056 | bytes 33316864 | tf_op jit(solution)/shard_map/hqk,qhd->khd/dot_general | solution.py:147
  762.1 10.2 slice.407
  794.1 12.8 %slice.405 = bf16[11,512,1024]{2,1,0:T(8,128)(2,1)} slice(f32[12,512,1024]{2,1,0:T(8,128)} %get-tuple-element.98), slice={[1:12], [0:512], [0:1024]} | slice | bytes 23068672 | tf_op jit(solution)/shard_map/slice | solution.py:133
  806.9 10.1 slice.404
  848.9 7.8 add_convert_fusion.2
  857.4 13.4 %fusion.178 = f32[3072,768]{1,0:T(8,128)S(1)} fusion(bf16[2048,768]{1,0:T(8,128)(2,1)} %param.27, f32[1024,3072]{1,0:T(8,128)} %fusion.203, f32[3072]{0:T(1024)S(1)} %copy-done.131), kind=kOutput, calls=%fused_computation.344 | convolution fusion | flops 4863295488 | bytes 23605248 | tf_op jit(solution)/shard_map/tf,td->fd/dot_general | solution.py:235
  870.8 13.0 %add_convert_fusion = bf16[3072,768]{1,0:T(8,128)(2,1)} fusion(f32[3072,768]{1,0:T(8,128)S(1)} %fusion.178, bf16[2048,768]{1,0:T(8,128)(2,1)S(1)} %copy-done.77, f32[1024,3072]{1,0:T(8,128)} %fusion.204, f32[3072]{0:T(1024)S(1)} %copy-done.131), kind=kOutput, calls=%fused_computation.72 | convolution fusion | flops 4868014080 | bytes 28323840 | tf_op jit(solution)/shard_map/tf,td->fd/dot_general | solution.py:235
  885.6 9.0 fusion.222
  898.2 9.0 fusion.223
  913.7 7.6 fusion.202
  921.4 10.0 add_convert_fusion.1
  946.3 59.1 %all-reduce.12 = (bf16[768]{0:T(1024)(128)(2,1)S(1)}, bf16[768]{0:T(1024)(128)(2,1)S(1)}, bf16[768]{0:T(1024)(128)(2,1)S(1)}, bf16[768]{0:T(1024)(128)(2,1)S(1)}...) all-reduce(bf16[768]{0:T(1024)(128)(2,1)S(1)} %dynamic-update-slice, ...), channel_id=1, replica_groups=mesh['fsdp'=16,'rep'=2] {'fsdp'}, use_global_device_ids=true, to_apply=%add.5 | all-reduce | flops 7680 | bytes 30720
  1005.4 12.4 %add_convert_fusion.5 = bf16[1024,768]{0,1:T(8,128)(2,1)} fusion(f32[1024,768]{0,1:T(8,128)} %copy-done.22, bf16[3072,768]{1,0:T(8,128)(2,1)} %all-gather.11.cloned.1.call-done, f32[768]{0:T(1024)S(1)} %convert_element_type.392, f32[1024,3072]{1,0:T(8,128)} %fusion.204, f32[3072]{0:T(1024)S(1)} %copy-done.131), kind=kOutput, calls=%fused_computation.135 | convolution fusion | flops 4865654784 | bytes 22035456 | tf_op jit(solution)/shard_map/dot_general | solution.py:189
  1017.8 62.9 %reduce-scatter.9.cloned.1.call-done = bf16[48,3072]{1,0:T(8,128)(2,1)} async-done(((bf16[768,3072]{1,0:T(8,128)(2,1)}), bf16[48,3072]{1,0:T(8,128)(2,1)}) %reduce-scatter.9.cloned.1.call-update) | async-done | bytes 294928 | tf_op jit(solution)/shard_map/reduce_scatter | solution.py:320
  1080.8 11.9 %add_convert_fusion.7 = bf16[1024,768]{0,1:T(8,128)(2,1)} fusion(f32[1024,768]{0,1:T(8,128)S(1)} %copy-done.21, bf16[3072,768]{1,0:T(8,128)(2,1)} %all-gather.11.cloned.1.call-done, f32[768]{0:T(1024)S(1)} %convert_element_type.392, f32[1024,3072]{1,0:T(8,128)} %fusion.203, f32[3072]{0:T(1024)S(1)} %copy-done.131), kind=kOutput, calls=%fused_computation.138 | convolution fusion | flops 4865654784 | bytes 22035456 | tf_op jit(solution)/shard_map/dot_general | solution.py:189
  (529 shorter events, 307.0 us)
Async XLA Ops:
  7.2 92.1 %all-gather.5.cloned.1.call-start = ((), (), s32[]{:S(2)}) async-start(), calls=%async_computation.4 | async-start | bytes 3760128 | tf_op jit(solution)/shard_map/all_gather | solution.py:359
  7.9 352.8 %all-gather.7.cloned.1.call-start = ((), (), s32[]{:S(2)}) async-start(), calls=%async_computation.5 | async-start | bytes 1253376 | tf_op jit(solution)/shard_map/all_gather | solution.py:360
  8.7 362.6 %all-gather.9.cloned.1.call-start = ((), (), s32[]{:S(2)}) async-start(), calls=%async_computation.6 | async-start | bytes 5013504 | tf_op jit(solution)/shard_map/all_gather | solution.py:361
  9.4 373.0 %all-gather.11.cloned.1.call-start = ((), (), s32[]{:S(2)}) async-start(), calls=%async_computation.7 | async-start | bytes 5013504 | tf_op jit(solution)/shard_map/all_gather | solution.py:362
  10.0 1007.8 %reduce-scatter.7.cloned.1.call-start = ((), (), s32[]{:S(2)}) async-start(), calls=%async_computation.9 | async-start | bytes 1253376 | tf_op jit(solution)/shard_map/reduce_scatter | solution.py:320
  81.4 56.2 %copy-start.134 = (f32[768]{0:T(1024)}, f32[768]{0:T(1024)S(1)}, u32[]{:S(2)}) copy-start(f32[768]{0:T(1024)S(1)} %convert_element_type.371) | copy-start | bytes 9220
  81.4 56.2 %copy-start.111 = (f32[768]{0:T(1024)}, f32[768]{0:T(1024)S(1)}, u32[]{:S(2)}) copy-start(f32[768]{0:T(1024)S(1)} %convert_element_type.370) | copy-start | bytes 9220
  89.6 48.0 %copy-start.14 = (bf16[1024,768]{0,1:T(8,128)(2,1)}, bf16[1024,768]{0,1:T(8,128)(2,1)S(1)}, u32[]{:S(2)}) copy-start(bf16[1024,768]{0,1:T(8,128)(2,1)S(1)} %copy.107) | copy-start | bytes 4718596
  90.0 47.7 %copy-start.109 = (f32[1024]{0:T(1024)}, f32[1024]{0:T(1024)S(1)}, u32[]{:S(2)}) copy-start(f32[1024]{0:T(1024)S(1)} %get-tuple-element.183) | copy-start | bytes 12292
  92.1 45.5 %copy-start.115 = (f32[1024]{0:T(1024)}, f32[1024]{0:T(1024)S(1)}, u32[]{:S(2)}) copy-start(f32[1024]{0:T(1024)S(1)} %fusion.156) | copy-start | bytes 12292
  113.7 13.6 %copy-start.10 = (bf16[1024,2304]{0,1:T(8,128)(2,1)S(1)}, bf16[1024,2304]{0,1:T(8,128)(2,1)}, u32[]{:S(2)}) copy-start(bf16[1024,2304]{0,1:T(8,128)(2,1)} %copy.87) | copy-start | bytes 14155780
  155.5 16.3 %copy-start.1 = (f32[12,512,1024]{2,1,0:T(8,128)}, f32[12,512,1024]{2,1,0:T(8,128)S(1)}, u32[]{:S(2)}) copy-start(f32[12,512,1024]{2,1,0:T(8,128)S(1)} %broadcast_multiply_fusion) | copy-start | bytes 75497472
  163.6 325.6 %copy-start.37 = (pred[512,1024]{1,0:T(8,128)(4,1)}, pred[512,1024]{1,0:T(8,128)(4,1)S(1)}, u32[]{:S(2)}) copy-start(pred[512,1024]{1,0:T(8,128)(4,1)S(1)} %get-tuple-element.143) | copy-start | bytes 1572868
  180.6 16.9 %copy-start = (f32[12,512,1024]{2,1,0:T(8,128)}, f32[12,512,1024]{2,1,0:T(8,128)S(1)}, u32[]{:S(2)}) copy-start(f32[12,512,1024]{2,1,0:T(8,128)S(1)} %broadcast_multiply_fusion.1) | copy-start | bytes 75497472
  195.4 21.2 %slice-start = ((s8[25165824]{0:T(1024)(128)(4,1)}), s8[4194304]{0:T(1024)(128)(4,1)S(1)}, s32[]{:S(2)}) async-start(s8[25165824]{0:T(1024)(128)(4,1)} %bitcast.273), calls=%async_computation.13 | async-start | bytes 8388608
  197.5 19.2 %slice-start.1 = ((s8[25165824]{0:T(1024)(128)(4,1)}), s8[4194304]{0:T(1024)(128)(4,1)S(1)}, s32[]{:S(2)}) async-start(s8[25165824]{0:T(1024)(128)(4,1)} %bitcast.273), calls=%async_computation.14 | async-start | bytes 8388608
  199.6 17.1 %slice-start.2 = ((s8[25165824]{0:T(1024)(128)(4,1)}), s8[4194304]{0:T(1024)(128)(4,1)S(1)}, s32[]{:S(2)}) async-start(s8[25165824]{0:T(1024)(128)(4,1)} %bitcast.273), calls=%async_computation.15 | async-start | bytes 8388608
  216.7 26.5 %slice-start.6 = ((s8[25165824]{0:T(1024)(128)(4,1)}), s8[4194304]{0:T(1024)(128)(4,1)S(1)}, s32[]{:S(2)}) async-start(s8[25165824]{0:T(1024)(128)(4,1)} %bitcast.275), calls=%async_computation.19 | async-start | bytes 8388608
  216.8 26.5 %slice-start.7 = ((s8[25165824]{0:T(1024)(128)(4,1)}), s8[4194304]{0:T(1024)(128)(4,1)S(1)}, s32[]{:S(2)}) async-start(s8[25165824]{0:T(1024)(128)(4,1)} %bitcast.275), calls=%async_computation.20 | async-start | bytes 8388608
  216.8 26.5 %slice-start.8 = ((s8[25165824]{0:T(1024)(128)(4,1)}), s8[4194304]{0:T(1024)(128)(4,1)S(1)}, s32[]{:S(2)}) async-start(s8[25165824]{0:T(1024)(128)(4,1)} %bitcast.275), calls=%async_computation.21 | async-start | bytes 8388608
  226.3 17.0 %slice-start.9 = ((s8[25165824]{0:T(1024)(128)(4,1)}), s8[4194304]{0:T(1024)(128)(4,1)S(1)}, s32[]{:S(2)}) async-start(s8[25165824]{0:T(1024)(128)(4,1)} %bitcast.275), calls=%async_computation.22 | async-start | bytes 8388608
  250.5 13.3 %copy-start.103 = (f32[12,512]{1,0:T(8,128)}, f32[12,512]{1,0:T(8,128)S(1)}, u32[]{:S(2)}) copy-start(f32[12,512]{1,0:T(8,128)S(1)} %log_add_fusion.2) | copy-start | bytes 73732
  250.5 13.3 %copy-start.59 = (pred[512,1024]{1,0:T(32,128)(4,1)S(1)}, pred[512,1024]{1,0:T(32,128)(4,1)}, u32[]{:S(2)}) copy-start(pred[512,1024]{1,0:T(32,128)(4,1)} %copy-done.58) | copy-start | bytes 1572868
  267.0 222.2 %copy-start.2 = (f32[512,1024]{1,0:T(8,128)}, f32[512,1024]{1,0:T(8,128)S(1)}, u32[]{:S(2)}) copy-start(f32[512,1024]{1,0:T(8,128)S(1)} %add_add_fusion.9) | copy-start | bytes 6291460
  290.3 198.8 %copy-start.97 = (f32[12,512]{1,0:T(8,128)}, f32[12,512]{1,0:T(8,128)S(1)}, u32[]{:S(2)}) copy-start(f32[12,512]{1,0:T(8,128)S(1)} %log_add_fusion.3) | copy-start | bytes 73732
  306.7 38.6 %copy-start.4 = (f32[512,1024]{1,0:T(8,128)}, f32[512,1024]{1,0:T(8,128)S(1)}, u32[]{:S(2)}) copy-start(f32[512,1024]{1,0:T(8,128)S(1)} %add_add_fusion.7) | copy-start | bytes 6291460
  364.6 90.5 %copy-start.93 = (f32[1024]{0:T(1024)}, f32[1024]{0:T(1024)S(1)}, u32[]{:S(2)}) copy-start(f32[1024]{0:T(1024)S(1)} %broadcast_multiply_fusion.4) | copy-start | bytes 12292
  366.2 88.9 %copy-start.105 = (f32[1024]{0:T(1024)}, f32[1024]{0:T(1024)S(1)}, u32[]{:S(2)}) copy-start(f32[1024]{0:T(1024)S(1)} %fusion.157) | copy-start | bytes 12292
  369.2 85.9 %copy-start.95 = (f32[1024]{0:T(1024)}, f32[1024]{0:T(1024)S(1)}, u32[]{:S(2)}) copy-start(f32[1024]{0:T(1024)S(1)} %broadcast_multiply_fusion.6) | copy-start | bytes 12292
  371.2 83.9 %copy-start.107 = (f32[1024]{0:T(1024)}, f32[1024]{0:T(1024)S(1)}, u32[]{:S(2)}) copy-start(f32[1024]{0:T(1024)S(1)} %fusion.155) | copy-start | bytes 12292
  382.4 17.1 %copy-start.46 = (bf16[768,3072]{1,0:T(8,128)(2,1)S(1)}, bf16[768,3072]{1,0:T(8,128)(2,1)}, u32[]{:S(2)}) copy-start(bf16[768,3072]{1,0:T(8,128)(2,1)} %all-gather.9.cloned.1.call-done) | copy-start | bytes 14155780
  410.4 27.0 %slice-start.20 = ((s8[4718592]{0:T(1024)(128)(4,1)}), s8[4194304]{0:T(1024)(128)(4,1)S(1)}, s32[]{:S(2)}) async-start(s8[4718592]{0:T(1024)(128)(4,1)} %bitcast.305), calls=%async_computation.33 | async-start | bytes 8388608
  421.8 15.7 %slice-start.21 = ((s8[4718592]{0:T(1024)(128)(4,1)}), s8[524288]{0:T(1024)(128)(4,1)S(1)}, s32[]{:S(2)}) async-start(s8[4718592]{0:T(1024)(128)(4,1)} %bitcast.305), calls=%async_computation.34 | async-start | bytes 1048576
  467.4 21.7 %copy-start.70 = (bf16[512,768]{0,1:T(8,128)(2,1)}, bf16[512,768]{0,1:T(8,128)(2,1)S(1)}, u32[]{:S(2)}) copy-start(bf16[512,768]{0,1:T(8,128)(2,1)S(1)} %get-tuple-element.121) | copy-start | bytes 2359300
  611.1 24.6 %copy-start.72 = (bf16[512,768]{0,1:T(8,128)(2,1)}, bf16[512,768]{0,1:T(8,128)(2,1)S(1)}, u32[]{:S(2)}) copy-start(bf16[512,768]{0,1:T(8,128)(2,1)S(1)} %get-tuple-element.119) | copy-start | bytes 2359300
  732.7 15.2 %copy-start.3 = (f32[512,1024]{1,0:T(8,128)S(1)}, f32[512,1024]{1,0:T(8,128)}, u32[]{:S(2)}) copy-start(f32[512,1024]{1,0:T(8,128)} %copy-done.2) | copy-start | bytes 6291460
  732.8 15.2 %copy-start.38 = (pred[512,1024]{1,0:T(8,128)(4,1)S(1)}, pred[512,1024]{1,0:T(8,128)(4,1)}, u32[]{:S(2)}) copy-start(pred[512,1024]{1,0:T(8,128)(4,1)} %copy-done.37) | copy-start | bytes 1572868
  732.8 15.2 %copy-start.98 = (f32[12,512]{1,0:T(8,128)S(1)}, f32[12,512]{1,0:T(8,128)}, u32[]{:S(2)}) copy-start(f32[12,512]{1,0:T(8,128)} %copy-done.97) | copy-start | bytes 73732
  732.8 285.0 %reduce-scatter.5.cloned.1.call-start = ((), (), s32[]{:S(2)}) async-start(), calls=%async_computation.8 | async-start | bytes 3760128 | tf_op jit(solution)/shard_map/reduce_scatter | solution.py:320
  732.8 15.1 %copy-start.71 = (bf16[512,768]{0,1:T(8,128)(2,1)S(1)}, bf16[512,768]{0,1:T(8,128)(2,1)}, u32[]{:S(2)}) copy-start(bf16[512,768]{0,1:T(8,128)(2,1)} %copy-done.70) | copy-start | bytes 2359300
  732.8 42.3 %slice-start.18 = ((s8[4718592]{0:T(1024)(128)(4,1)}), s8[4194304]{0:T(1024)(128)(4,1)S(1)}, s32[]{:S(2)}) async-start(s8[4718592]{0:T(1024)(128)(4,1)} %bitcast.301), calls=%async_computation.31 | async-start | bytes 8388608
  747.9 27.2 %slice-start.19 = ((s8[4718592]{0:T(1024)(128)(4,1)}), s8[524288]{0:T(1024)(128)(4,1)S(1)}, s32[]{:S(2)}) async-start(s8[4718592]{0:T(1024)(128)(4,1)} %bitcast.301), calls=%async_computation.32 | async-start | bytes 1048576
  794.1 25.7 %slice-start.14 = ((s8[4718592]{0:T(1024)(128)(4,1)}), s8[4194304]{0:T(1024)(128)(4,1)S(1)}, s32[]{:S(2)}) async-start(s8[4718592]{0:T(1024)(128)(4,1)} %bitcast.285), calls=%async_computation.27 | async-start | bytes 8388608
  856.7 161.1 %reduce-scatter.11.cloned.1.call-start = ((), (), s32[]{:S(2)}) async-start(), calls=%async_computation.11 | async-start | bytes 5013504 | tf_op jit(solution)/shard_map/reduce_scatter | solution.py:320
  857.4 13.4 %copy-start.77 = (bf16[2048,768]{1,0:T(8,128)(2,1)S(1)}, bf16[2048,768]{1,0:T(8,128)(2,1)}, u32[]{:S(2)}) copy-start(bf16[2048,768]{1,0:T(8,128)(2,1)} %param.27) | copy-start | bytes 9437188
  883.8 196.9 %reduce-scatter.9.cloned.1.call-start = ((), (), s32[]{:S(2)}) async-start(), calls=%async_computation.10 | async-start | bytes 5013504 | tf_op jit(solution)/shard_map/reduce_scatter | solution.py:320
  931.4 188.0 %all-reduce.18.cloned.1.call-start = ((), (), s32[]{:S(2)}) async-start(), calls=%async_computation.12 | async-start | bytes 1769472 | tf_op jit(solution)/shard_map/psum | solution.py:389
  1005.4 75.4 %copy-start.21 = (f32[1024,768]{0,1:T(8,128)S(1)}, f32[1024,768]{0,1:T(8,128)}, u32[]{:S(2)}) copy-start(f32[1024,768]{0,1:T(8,128)} %copy-done.18) | copy-start | bytes 9437188
  (132 other events, 762.0 us)
Sparse Core Ops, SparseCore 0:
  10.3 50.2 all-gather.4
  62.9 37.3 all-gather.6
  102.6 52.1 all-gather.8
  156.9 51.7 all-gather.10
  732.9 55.4 reduce-scatter.6
  856.8 65.5 reduce-scatter.4
  926.2 74.9 reduce-scatter.10
  1006.1 74.5 reduce-scatter.8
  1083.3 36.1 all-reduce.17
where the time goes:
time: 1140 us; the launch traced here: 1130 us
  matrix products  534 us (47%)
  other arithmetic  257 us (23%)
  blocking collectives  128 us (11%)
  local copies, waits for them, and re-layouts  127 us (11%)
  waiting for transfers between devices  69 us (6%)
  between operations  19.1 us (2%)
    unnamed x2, blocking collectives  123 us
    dot_general x4, matrix products, attend_back(): jnp.einsum('qhd,khd->hqk', grad_block, value_rows, preferred_element_type...  87.5 us
    reduce_scatter x4, waiting for transfers between devices, run_batches(): lax.psum_scatter(as_sent(summed_grads), 'fsdp', scatter_dimension=0, tile...  62.9 us
    dot_general x4, matrix products, attend_back(): jnp.einsum('hqk,qhd->khd', attention.astype(jnp.bfloat16), grad_block, pr...  55.6 us
    dot_general x4, matrix products, attend(): jnp.einsum('hqk,khd->qhd', attention, value_rows, preferred_element_type=...  51.8 us
    reduce_sum x2, other arithmetic, attend_back(): later_sum = later_sum + jnp.sum(grad_penalty, axis=0)  51.3 us
    reduce_sum x2, other arithmetic, attend_back(): grad_penalty = -jnp.sum(grad_logits, axis=0)  50 us
    unnamed x368, local copies, waits for them, and re-layouts  49.8 us
  transfers between devices with their start and end apart: 9, of which 2 were waited for; matrix products, arithmetic and copies ran while one was open for 48% of the time, Pallas kernels for 0%

commit v1 on v0

v1 whole, which is shorter than its diff:
```python
import functools

import jax
import jax.numpy as jnp
from jax import lax
from jax.experimental import pallas as pl
from jax.experimental.pallas import tpu as pltpu
from jax.sharding import PartitionSpec as P

HEAD_DIM = 64
PAIR = 2 * HEAD_DIM
ROWS = 256
MASKED_VALUE = -1e30
EPSILON = 1e-05
SCALE = HEAD_DIM**-0.5
GELU_IN = 0.7978845608028654
GELU_CUBE = 0.044715
VMEM_LIMIT = 60 * 1024 * 1024

F32 = jnp.float32
BF16 = jnp.bfloat16


def dot(left, right):
    return lax.dot_general(left, right, (((1,), (0,)), ((), ())), preferred_element_type=F32)


def dot_nt(left, right):
    return lax.dot_general(left, right, (((1,), (1,)), ((), ())), preferred_element_type=F32)


def dot_tn(left, right):
    return lax.dot_general(left, right, (((0,), (0,)), ((), ())), preferred_element_type=F32)


def row_mean(values):
    return jnp.mean(values, axis=-1, keepdims=True)


def normalize(values):
    center = values - row_mean(values)
    inverse = lax.rsqrt(row_mean(center * center) + EPSILON)
    return (center * inverse, inverse)


def norm_back(grad, normed, inverse):
    return (grad - row_mean(grad) - normed * row_mean(grad * normed)) * inverse


def column_sum(values):
    return jnp.sum(values, axis=0, keepdims=True)


def params(*semantics):
    return pltpu.CompilerParams(dimension_semantics=semantics, vmem_limit_bytes=VMEM_LIMIT)


def project_kernel(x_ref, gain_ref, shift_ref, w_ref, o_ref):
    normed, _ = normalize(x_ref[...].astype(F32))
    normed = (normed * gain_ref[...] + shift_ref[...]).astype(BF16)
    o_ref[...] = dot(normed, w_ref[...]).astype(BF16)


def project(tokens, gain, shift, weight):
    count, width = tokens.shape
    columns = weight.shape[1]
    block = 512
    return pl.pallas_call(
        project_kernel,
        out_shape=jax.ShapeDtypeStruct((count, columns), BF16),
        grid=(count // block,),
        in_specs=[
            pl.BlockSpec((block, width), lambda i: (i, 0)),
            pl.BlockSpec((1, width), lambda i: (0, 0)),
            pl.BlockSpec((1, width), lambda i: (0, 0)),
            pl.BlockSpec((width, columns), lambda i: (0, 0)),
        ],
        out_specs=pl.BlockSpec((block, columns), lambda i: (i, 0)),
        compiler_params=params("arbitrary"),
        name="project",
    )(tokens, gain, shift, weight)


def label_of(position, start_ref, length_ref, seq, pieces):
    label = jnp.zeros(position.shape, jnp.int32)
    for piece in range(pieces):
        start = start_ref[seq, piece]
        inside = (position >= start) & (position < start + length_ref[seq, piece])
        label = jnp.where(inside, piece + 1, label)
    return label


def key_count(first_row, slot):
    return (first_row // slot + 1) * slot


def block_masks(start_ref, length_ref, seq, pieces, first_row, keys):
    query_pos = first_row + lax.broadcasted_iota(jnp.int32, (ROWS, 1), 0)
    key_pos = lax.broadcasted_iota(jnp.int32, (1, keys), 1)
    query_label = label_of(query_pos, start_ref, length_ref, seq, pieces)
    key_label = label_of(key_pos, start_ref, length_ref, seq, pieces)
    query_label = jnp.where(query_label > 0, query_label, -1)
    allowed = (key_pos <= query_pos) | (query_label == key_label)
    chosen = allowed & (key_pos != 0) & (key_pos != query_pos)
    return (allowed, chosen)


def triangle_sum(triangle, values):
    upper = values.astype(BF16)
    rest = values - upper.astype(F32)
    middle = rest.astype(BF16)
    lower = (rest - middle.astype(F32)).astype(BF16)
    return dot(triangle, upper) + dot(triangle, middle) + dot(triangle, lower)


def head_mask(half):
    lane = lax.broadcasted_iota(jnp.int32, (1, PAIR), 1)
    return (lane >= HEAD_DIM) if half else (lane < HEAD_DIM)


def attend_kernel(
    slot, pieces, start_ref, length_ref, q_ref, k_ref, v_ref, o_ref, *rest
):
    att_refs, (bias_ref, prefix_ref) = rest[:-2], rest[-2:]
    seq = pl.program_id(0)
    length = q_ref.shape[0]
    zero = jnp.zeros((), BF16)

    @pl.when(pl.program_id(1) == 0)
    def _():
        prefix_ref[...] = jnp.zeros_like(prefix_ref)
        row = lax.broadcasted_iota(jnp.int32, (ROWS, ROWS), 0)
        col = lax.broadcasted_iota(jnp.int32, (ROWS, ROWS), 1)
        triangle = (col < row).astype(BF16)
        for first_row in range(0, length, ROWS):
            keys = key_count(first_row, slot)
            rows = pl.ds(first_row, ROWS)
            query = jnp.where(head_mask(0), q_ref[rows, :], zero)
            scores = dot_nt(query, k_ref[:keys, :]) * SCALE
            allowed, chosen = block_masks(start_ref, length_ref, seq, pieces, first_row, keys)
            selected = jnp.where(chosen & (scores > 0), scores, 0.0)
            penalty = prefix_ref[:, :keys] + triangle_sum(triangle, selected)
            bias_ref[rows, :keys] = jnp.where(allowed, -penalty, MASKED_VALUE)
            prefix_ref[:, :keys] += column_sum(selected)

    for first_row in range(0, length, ROWS):
        keys = key_count(first_row, slot)
        rows = pl.ds(first_row, ROWS)
        slot_rows = pl.ds(first_row % slot, ROWS)
        mixed = None
        for half in range(2):
            mask = head_mask(half)
            query = jnp.where(mask, q_ref[rows, :], zero) * jnp.asarray(SCALE, BF16)
            logits = dot_nt(query, k_ref[:keys, :]) + bias_ref[rows, :keys]
            largest = jnp.max(logits, axis=-1, keepdims=True)
            raised = jnp.exp(logits - largest)
            inverse = 1.0 / jnp.sum(raised, axis=-1, keepdims=True)
            attention = (raised * inverse).astype(BF16)
            att_refs[first_row // slot][half, slot_rows, :] = attention
            value = jnp.where(mask, v_ref[:keys, :], zero)
            part = dot(attention, value)
            mixed = part if mixed is None else mixed + part
        o_ref[rows, :] = mixed.astype(BF16)


def attend(projected, starts, lengths):
    sequences, pieces = starts.shape
    count, columns = projected.shape
    length = count // sequences
    slot = length // pieces
    width = columns // 3
    pairs = width // PAIR

    def part(which):
        return pl.BlockSpec((length, PAIR), lambda s, p, a, b: (s, which * pairs + p))

    att_shapes = [
        jax.ShapeDtypeStruct((sequences, 2 * pairs, slot, (i + 1) * slot), BF16)
        for i in range(pieces)
    ]
    att_specs = [
        pl.BlockSpec((None, 2, slot, (i + 1) * slot), lambda s, p, a, b: (s, p, 0, 0))
        for i in range(pieces)
    ]
    results = pl.pallas_call(
        functools.partial(attend_kernel, slot, pieces),
        out_shape=[jax.ShapeDtypeStruct((count, width), BF16)] + att_shapes,
        grid_spec=pltpu.PrefetchScalarGridSpec(
            num_scalar_prefetch=2,
            grid=(sequences, pairs),
            in_specs=[part(0), part(1), part(2)],
            out_specs=[pl.BlockSpec((length, PAIR), lambda s, p, a, b: (s, p))] + att_specs,
            scratch_shapes=[
                pltpu.VMEM((length, length), F32),
                pltpu.VMEM((1, length), F32),
            ],
        ),
        compiler_params=params("arbitrary", "arbitrary"),
        name="attend",
    )(starts, lengths, projected, projected, projected)
    return (results[0], results[1:])


def attend_back_kernel(
    slot, pieces, start_ref, length_ref, q_ref, k_ref, v_ref, gm_ref, o_ref, *rest
):
    att_refs = rest[:pieces]
    gq_ref, gk_ref, gv_ref, sum_ref, later_ref, dq_ref, dk_ref, dv_ref = rest[pieces:]
    seq, step = pl.program_id(0), pl.program_id(1)
    last = step == pl.num_programs(1) - 1
    length = q_ref.shape[0]
    zero = jnp.zeros((), BF16)
    scale = jnp.asarray(SCALE, BF16)

    @pl.when(step == 0)
    def _():
        sum_ref[...] = jnp.zeros_like(sum_ref)

    dk_ref[...] = jnp.zeros_like(dk_ref)
    dv_ref[...] = jnp.zeros_like(dv_ref)

    def head(half, first_head):
        mask = head_mask(half)
        if first_head:
            later_ref[...] = jnp.zeros_like(later_ref)
            row = lax.broadcasted_iota(jnp.int32, (ROWS, ROWS), 0)
            col = lax.broadcasted_iota(jnp.int32, (ROWS, ROWS), 1)
            triangle = (col > row).astype(BF16)
        for first_row in reversed(range(0, length, ROWS)):
            keys = key_count(first_row, slot)
            rows = pl.ds(first_row, ROWS)
            slot_rows = pl.ds(first_row % slot, ROWS)
            grad = jnp.where(mask, gm_ref[rows, :], zero)
            delta = jnp.sum(
                grad.astype(F32) * o_ref[rows, :].astype(F32), axis=-1, keepdims=True
            )
            attention = att_refs[first_row // slot][half, slot_rows, :]
            grad_attention = dot_nt(grad, v_ref[:keys, :])
            grad_logits = attention.astype(F32) * (grad_attention - delta)
            query = jnp.where(mask, q_ref[rows, :], zero) * scale
            if first_head:
                total = sum_ref[rows, :keys] + grad_logits
                grad_selected = -(later_ref[:, :keys] + triangle_sum(triangle, total))
                later_ref[:, :keys] += column_sum(total)
                _, chosen = block_masks(start_ref, length_ref, seq, pieces, first_row, keys)
                positive = dot_nt(query, k_ref[:keys, :]) > 0
                grad_logits = grad_logits + jnp.where(chosen & positive, grad_selected, 0.0)
            else:
                sum_ref[rows, :keys] += grad_logits
            grad_scores = grad_logits.astype(BF16)
            key = jnp.where(mask, k_ref[:keys, :], zero) * scale
            part = dot(grad_scores, key)
            if half == 1:
                dq_ref[rows, :] = part
            else:
                dq_ref[rows, :] += part
            dk_ref[:keys, :] += dot_tn(grad_scores, query)
            dv_ref[:keys, :] += dot_tn(attention, grad)

    head(1, False)

    @pl.when(jnp.logical_not(last))
    def _():
        head(0, False)

    @pl.when(last)
    def _():
        head(0, True)

    gq_ref[...] = dq_ref[...].astype(BF16)
    gk_ref[...] = dk_ref[...].astype(BF16)
    gv_ref[...] = dv_ref[...].astype(BF16)


def attend_back(projected, starts, lengths, grad_mixed, mixed, attention):
    sequences, pieces = starts.shape
    count, columns = projected.shape
    length = count // sequences
    slot = length // pieces
    width = columns // 3
    pairs = width // PAIR

    def part(which):
        return pl.BlockSpec(
            (length, PAIR), lambda s, p, a, b: (s, which * pairs + pairs - 1 - p)
        )

    att_specs = [
        pl.BlockSpec(
            (None, 2, slot, (i + 1) * slot), lambda s, p, a, b: (s, pairs - 1 - p, 0, 0)
        )
        for i in range(pieces)
    ]
    return pl.pallas_call(
        functools.partial(attend_back_kernel, slot, pieces),
        out_shape=[jax.ShapeDtypeStruct((count, width), BF16)] * 3,
        grid_spec=pltpu.PrefetchScalarGridSpec(
            num_scalar_prefetch=2,
            grid=(sequences, pairs),
            in_specs=[part(0), part(1), part(2), part(0), part(0)] + att_specs,
            out_specs=[part(0), part(0), part(0)],
            scratch_shapes=[
                pltpu.VMEM((length, length), F32),
                pltpu.VMEM((1, length), F32),
                pltpu.VMEM((length, PAIR), F32),
                pltpu.VMEM((length, PAIR), F32),
                pltpu.VMEM((length, PAIR), F32),
            ],
        ),
        compiler_params=params("arbitrary", "arbitrary"),
        name="attend_back",
    )(starts, lengths, projected, projected, projected, grad_mixed, mixed, *attention)


def gelu_and_slope(values):
    square = values * values
    inner = GELU_IN * values * (1.0 + GELU_CUBE * square)
    bent = jnp.tanh(inner)
    half = 0.5 * (1.0 + bent)
    slope = half + 0.5 * values * (1.0 - bent * bent) * (
        GELU_IN * (1.0 + 3.0 * GELU_CUBE * square)
    )
    return (values * half, slope)


def feed_kernel(
    chunk,
    x_ref,
    mixed_ref,
    cot_ref,
    gain_ref,
    shift_ref,
    up_bias_ref,
    down_bias_ref,
    wo_hbm,
    wu_hbm,
    wd_hbm,
    out_ref,
    gmid_ref,
    gmix_ref,
    small_ref,
    gwo_hbm,
    gwu_hbm,
    gwd_hbm,
    wo_ref,
    wu_ref,
    wd_ref,
    gwo_ref,
    gwu_ref,
    gwd_ref,
    acc_ref,
    gnorm_ref,
    n2_ref,
    mid_ref,
    stage_ref,
    load_sem,
    stage_sem,
):
    step = pl.program_id(0)
    steps = pl.num_programs(0)
    chunks = wu_ref.shape[0]
    width = x_ref.shape[1]

    def load_out():
        return pltpu.make_async_copy(wo_hbm, wo_ref, load_sem.at[0])

    def load_up(c):
        return pltpu.make_async_copy(
            wu_hbm.at[:, pl.ds(c * chunk, chunk)], wu_ref.at[c], load_sem.at[1]
        )

    def load_down(c):
        return pltpu.make_async_copy(
            wd_hbm.at[pl.ds(c * chunk, chunk), :], wd_ref.at[c], load_sem.at[2]
        )

    @pl.when(step == 0)
    def _():
        load_out().start()
        for c in range(chunks):
            load_up(c).start()
        for c in range(chunks):
            load_down(c).start()
        gwo_ref[...] = jnp.zeros_like(gwo_ref)
        gwu_ref[...] = jnp.zeros_like(gwu_ref)
        gwd_ref[...] = jnp.zeros_like(gwd_ref)
        small_ref[...] = jnp.zeros_like(small_ref)
        load_out().wait()

    mid_ref[...] = x_ref[...].astype(F32) + dot(mixed_ref[...], wo_ref[...])

    @pl.when(step == 0)
    def _():
        for c in range(chunks):
            load_up(c).wait()
        for c in range(chunks):
            load_down(c).wait()

    normed, _ = normalize(mid_ref[...])
    n2_ref[...] = (normed * gain_ref[...] + shift_ref[...]).astype(BF16)
    acc_ref[...] = jnp.zeros_like(acc_ref)
    gnorm_ref[...] = jnp.zeros_like(gnorm_ref)

    def one_chunk(c, carry):
        before = dot(n2_ref[...], wu_ref[c]) + up_bias_ref[c]
        hidden, slope = gelu_and_slope(before)
        hidden = hidden.astype(BF16)
        acc_ref[...] += dot(hidden, wd_ref[c])
        gwd_ref[c] += dot_tn(hidden, cot_ref[...])
        grad_hidden = dot_nt(cot_ref[...], wd_ref[c]).astype(BF16)
        grad_before = (grad_hidden.astype(F32) * slope).astype(BF16)
        small_ref[3 + c] += column_sum(grad_before.astype(F32))
        gnorm_ref[...] += dot_nt(grad_before, wu_ref[c])
        gwu_ref[c] += dot_tn(n2_ref[...], grad_before)
        return carry

    lax.fori_loop(0, chunks, one_chunk, 0)

    out_ref[...] = (mid_ref[...] + (acc_ref[...] + down_bias_ref[...])).astype(BF16)
    grad_normed = gnorm_ref[...]
    normed, inverse = normalize(mid_ref[...])
    cot = cot_ref[...].astype(F32)
    small_ref[0] += column_sum(grad_normed * normed)
    small_ref[1] += column_sum(grad_normed)
    small_ref[2] += column_sum(cot)
    grad_middle = cot + norm_back(grad_normed * gain_ref[...], normed, inverse)
    gmid_ref[...] = grad_middle
    grad_proj = grad_middle.astype(BF16)
    gwo_ref[...] += dot_tn(mixed_ref[...], grad_proj)
    gmix_ref[...] = dot_nt(grad_proj, wo_ref[...]).astype(BF16)

    @pl.when(step == steps - 1)
    def _():
        copies = []

        def put(value, target):
            i = len(copies)
            if i >= 2:
                copies[i - 2].wait()
            stage_ref[i % 2] = value.astype(BF16)
            copy = pltpu.make_async_copy(stage_ref.at[i % 2], target, stage_sem.at[i % 2])
            copy.start()
            copies.append(copy)

        put(gwo_ref[...], gwo_hbm)
        for c in range(chunks):
            put(gwu_ref[c], gwu_hbm.at[:, pl.ds(c * chunk, chunk)])
            put(gwd_ref[c], gwd_hbm.at[pl.ds(c * chunk, chunk), :])
        copies[-2].wait()
        copies[-1].wait()


def feed(tokens, mixed, cotangent, gain, shift, up_bias, down_bias, wo, wu, wd):
    count, width = tokens.shape
    hidden = wu.shape[1]
    block = 512
    chunk = width
    chunks = hidden // chunk
    rows = pl.BlockSpec((block, width), lambda i: (i, 0))
    line = pl.BlockSpec((1, width), lambda i: (0, 0))
    anywhere = pl.BlockSpec(memory_space=pl.ANY)
    return pl.pallas_call(
        functools.partial(feed_kernel, chunk),
        out_shape=[
            jax.ShapeDtypeStruct((count, width), BF16),
            jax.ShapeDtypeStruct((count, width), F32),
            jax.ShapeDtypeStruct((count, width), BF16),
            jax.ShapeDtypeStruct((3 + chunks, 1, width), F32),
            jax.ShapeDtypeStruct(wo.shape, BF16),
            jax.ShapeDtypeStruct(wu.shape, BF16),
            jax.ShapeDtypeStruct(wd.shape, BF16),
        ],
        grid=(count // block,),
        in_specs=[
            rows,
            rows,
            rows,
            line,
            line,
            pl.BlockSpec((chunks, 1, chunk), lambda i: (0, 0, 0)),
            line,
            anywhere,
            anywhere,
            anywhere,
        ],
        out_specs=[
            rows,
            rows,
            rows,
            pl.BlockSpec((3 + chunks, 1, width), lambda i: (0, 0, 0)),
            anywhere,
            anywhere,
            anywhere,
        ],
        scratch_shapes=[
            pltpu.VMEM(wo.shape, BF16),
            pltpu.VMEM((chunks, width, chunk), BF16),
            pltpu.VMEM((chunks, chunk, width), BF16),
            pltpu.VMEM(wo.shape, F32),
            pltpu.VMEM((chunks, width, chunk), F32),
            pltpu.VMEM((chunks, chunk, width), F32),
            pltpu.VMEM((block, width), F32),
            pltpu.VMEM((block, width), F32),
            pltpu.VMEM((block, width), BF16),
            pltpu.VMEM((block, width), F32),
            pltpu.VMEM((2, width, chunk), BF16),
            pltpu.SemaphoreType.DMA((3,)),
            pltpu.SemaphoreType.DMA((2,)),
        ],
        compiler_params=params("arbitrary"),
        name="feed",
    )(
        tokens,
        mixed,
        cotangent,
        gain,
        shift,
        up_bias.reshape(chunks, 1, chunk),
        down_bias,
        wo,
        wu,
        wd,
    )


def input_kernel(
    x_ref,
    gmid_ref,
    gq_ref,
    gk_ref,
    gv_ref,
    gain_ref,
    shift_ref,
    w_ref,
    gx_ref,
    small_ref,
    gw_ref,
    acc_ref,
):
    step = pl.program_id(0)
    width = x_ref.shape[1]

    @pl.when(step == 0)
    def _():
        acc_ref[...] = jnp.zeros_like(acc_ref)
        small_ref[...] = jnp.zeros_like(small_ref)

    normed, inverse = normalize(x_ref[...].astype(F32))
    low = (normed * gain_ref[...] + shift_ref[...]).astype(BF16)
    grad_normed = None
    for which, ref in enumerate((gq_ref, gk_ref, gv_ref)):
        grad = ref[...]
        acc_ref[which] += dot_tn(low, grad)
        part = dot_nt(grad, w_ref[:, which * width : (which + 1) * width])
        grad_normed = part if grad_normed is None else grad_normed + part
    small_ref[0] += column_sum(grad_normed * normed)
    small_ref[1] += column_sum(grad_normed)
    gx_ref[...] = gmid_ref[...] + norm_back(grad_normed * gain_ref[...], normed, inverse)

    @pl.when(step == pl.num_programs(0) - 1)
    def _():
        for which in range(3):
            gw_ref[:, which * width : (which + 1) * width] = acc_ref[which].astype(BF16)


def input_back(tokens, grad_middle, grads, gain, shift, weight):
    count, width = tokens.shape
    block = 512
    rows = pl.BlockSpec((block, width), lambda i: (i, 0))
    line = pl.BlockSpec((1, width), lambda i: (0, 0))
    return pl.pallas_call(
        input_kernel,
        out_shape=[
            jax.ShapeDtypeStruct((count, width), F32),
            jax.ShapeDtypeStruct((2, 1, width), F32),
            jax.ShapeDtypeStruct(weight.shape, BF16),
        ],
        grid=(count // block,),
        in_specs=[rows] * 5 + [line, line, pl.BlockSpec(weight.shape, lambda i: (0, 0))],
        out_specs=[
            rows,
            pl.BlockSpec((2, 1, width), lambda i: (0, 0, 0)),
            pl.BlockSpec(weight.shape, lambda i: (0, 0)),
        ],
        scratch_shapes=[pltpu.VMEM((3, width, width), F32)],
        compiler_params=params("arbitrary"),
        name="input_back",
    )(tokens, grad_middle, *grads, gain, shift, weight)


def gather(value):
    return lax.all_gather(value, "fsdp", axis=0, tiled=True)


def local(
    tokens,
    piece_start,
    piece_length,
    query_key_value,
    output_weight,
    up_weight,
    down_weight,
    first_gain,
    first_shift,
    second_gain,
    second_shift,
    up_bias,
    down_bias,
    cotangent,
):
    width = tokens.shape[1]
    vectors = (first_gain, first_shift, second_gain, second_shift, up_bias, down_bias)
    sizes = [v.shape[0] for v in vectors]
    total = sum(sizes)
    padded = -(-total // 1024) * 1024
    flat = jnp.pad(jnp.concatenate(vectors), (0, padded - total)).reshape(1, 8, padded // 8)
    flat = gather(flat).reshape(-1, padded)
    vectors, at = ([], 0)
    for size in sizes:
        vectors.append(flat[:, at : at + size].reshape(1, -1))
        at += size
    gain1, shift1, gain2, shift2, up_bias, down_bias = (v.astype(F32) for v in vectors)

    wqkv = gather(query_key_value)
    wo = gather(output_weight)
    wu = gather(up_weight)
    wd = gather(down_weight)

    projected = project(tokens, gain1, shift1, wqkv)
    mixed, attention = attend(projected, piece_start, piece_length)
    block_output, grad_middle, grad_mixed, small2, gwo, gwu, gwd = feed(
        tokens, mixed, cotangent, gain2, shift2, up_bias, down_bias, wo, wu, wd
    )
    grads = attend_back(projected, piece_start, piece_length, grad_mixed, mixed, attention)
    grad_tokens, small1, gwqkv = input_back(tokens, grad_middle, grads, gain1, shift1, wqkv)

    devices = lax.axis_size("fsdp")
    small = jnp.concatenate([small1.reshape(-1, width), small2.reshape(-1, width)], axis=0)

    def scatter(value):
        return lax.psum_scatter(value, "fsdp", scatter_dimension=0, tiled=True)

    def across(value):
        return lax.psum(value, "rep").astype(F32)

    small = small.astype(BF16)
    hidden = up_bias.shape[1]
    order = [small[0], small[1], small[2], small[3], small[5:].reshape(-1), small[4]]
    packed = jnp.concatenate([v.reshape(devices, -1) for v in order], axis=1)
    packed = jnp.pad(packed, ((0, 0), (0, padded - total))).reshape(devices * 8, padded // 8)
    packed = across(scatter(packed)).reshape(-1)
    tails, at = ([], 0)
    for size in sizes:
        tails.append(packed[at : at + size])
        at += size
    gfg, gfs, gsg, gss, gub, gdb = tails
    return (
        block_output,
        grad_tokens,
        across(scatter(gwqkv)),
        across(scatter(gwo)),
        across(scatter(gwu)),
        across(scatter(gwd)),
        gfg,
        gfs,
        gsg,
        gss,
        gub,
        gdb,
    )


def solution(mesh):
    rows = P(("fsdp", "rep"), None)
    matrix = P("fsdp", None)
    vector = P("fsdp")
    return jax.shard_map(
        local,
        mesh=mesh,
        in_specs=(rows,) * 3 + (matrix,) * 4 + (vector,) * 6 + (rows,),
        out_specs=(rows,) * 2 + (matrix,) * 4 + (vector,) * 6,
        check_vma=False,
    )
```

time: 1140 us -> 714 us (0.63)
  matrix products: 534 us -> 0 us
  Pallas kernels: 0 us -> 264 us
  waiting for transfers between devices: 69 us -> 323 us
  other arithmetic: 257 us -> 7.09 us
  local copies, waits for them, and re-layouts: 127 us -> 10.7 us
  blocking collectives: 128 us -> 86.3 us
    dot_general x72 -> x0, matrix products: 534 us -> none  [the longest x4 87.5 us: attend_back(): jnp.einsum('qhd,khd->hqk', grad_block, value_rows, preferred_element_type...]
    pallas_call x0 -> x5, Pallas kernels: none -> 264 us  [the longest x1 102 us: feed(): pl.pallas_call(functools.partial(feed_kernel, chunk), out_shape=[jax.Shap...]
    reduce_sum x21 -> x0, other arithmetic: 168 us -> none  [the longest x2 51.3 us: attend_back(): later_sum = later_sum + jnp.sum(grad_penalty, axis=0)]
    reduce_scatter x4, waiting for transfers between devices: 62.9 us -> 222 us  [scatter(): return lax.psum_scatter(value, 'fsdp', scatter_dimension=0, tiled=True)]
    all_gather x4, waiting for transfers between devices: 0.03 us -> 96.6 us  [gather(): return lax.all_gather(value, 'fsdp', axis=0, tiled=True)]
    unnamed x2 -> x1, blocking collectives: 123 us -> 58.1 us
    reduce_max x4 -> x0, other arithmetic: 49.4 us -> none  [attend(): largest = jnp.max(logits, axis=-1, keepdims=True)]
    unnamed x368 -> x8, local copies, waits for them, and re-layouts: 49.8 us -> 0.61 us
  transfers between devices with their start and end apart: 9 -> 9, of which waited for: 2 -> 6; matrix products, arithmetic and copies ran while one was open for 48% -> 2% of each run, Pallas kernels for 0% -> 23%
where the time goes in v1:
time: 714 us; the launch traced here: 707 us
  waiting for transfers between devices  323 us (45%)
  Pallas kernels  264 us (37%)
  blocking collectives  86.3 us (12%)
  between operations  15.1 us (2%)
  local copies, waits for them, and re-layouts  10.7 us (1%)
    reduce_scatter x4, waiting for transfers between devices, scatter(): return lax.psum_scatter(value, 'fsdp', scatter_dimension=0, tiled=True)  222 us
    pallas_call x1, Pallas kernels, feed(): pl.pallas_call(functools.partial(feed_kernel, chunk), out_shape=[jax.Shap...  102 us
    all_gather x4, waiting for transfers between devices, gather(): return lax.all_gather(value, 'fsdp', axis=0, tiled=True)  96.6 us
    pallas_call x1, Pallas kernels, attend_back(): pl.pallas_call(functools.partial(attend_back_kernel, slot, pieces), out_s...  65.5 us
    unnamed x1, blocking collectives  58.1 us
    pallas_call x1, Pallas kernels, attend(): pl.pallas_call(functools.partial(attend_kernel, slot, pieces), out_shape=...  56.8 us
    pallas_call x1, Pallas kernels, input_back(): pl.pallas_call(input_kernel, out_shape=[jax.ShapeDtypeStruct((count, widt...  26.9 us
    all_gather x1, blocking collectives, gather(): return lax.all_gather(value, 'fsdp', axis=0, tiled=True)  23.2 us
  transfers between devices with their start and end apart: 9, of which 6 were waited for; matrix products, arithmetic and copies ran while one was open for 2% of the time, Pallas kernels for 23%

profile of v1, /device:TPU:0, one launch (start us, length us, event | category | flops | bytes accessed | tf_op | source)
XLA Modules:
  0.0 707.1 jit_solution(18343467856198675992)
XLA Ops:
  7.2 0.7 all-gather.5.cloned.1.call-update
  8.0 0.7 all-gather.7.cloned.1.call-update
  8.7 0.7 all-gather.11.cloned.1.call-update
  9.4 0.5 all-gather.9.cloned.1.call-update
  10.0 0.0 reduce-scatter.7.cloned.1.call-start
  10.0 4.1 concatenate.8
  14.1 23.2 %all_gather.15 = bf16[16,8,128]{2,1,0:T(8,128)(2,1)S(1)} all-gather(bf16[1,8,128]{2,1,0:T(8,128)(2,1)S(1)} %pad_bitcast_fusion), channel_id=1, replica_groups=mesh['fsdp'=16,'rep'=2] {'fsdp'}, dimensions={0}, use_global_device_ids=true | all-gather | bytes 34816 | tf_op jit(solution)/shard_map/all_gather | solution.py:592
  37.4 0.1 slice_convert_fusion.1
  37.5 0.7 reshape.152.gain_ref
  38.1 0.7 reshape.153.shift_ref
  38.8 0.7 reshape.154.gain_ref
  39.5 0.7 reshape.155.shift_ref
  40.1 0.7 reshape.157.down_bias_ref
  40.8 0.1 slice_convert_fusion
  40.8 0.7 reshape.156.up_bias_ref
  41.5 18.4 %all-gather.5.cloned.1.call-done.w_ref = bf16[768,2304]{1,0:T(8,128)(2,1)} async-done(((bf16[48,2304]{1,0:T(8,128)(2,1)}), bf16[768,2304]{1,0:T(8,128)(2,1)}) %all-gather.5.cloned.1.call-update) | async-done | bytes 3538960 | tf_op jit(solution)/shard_map/all_gather | solution.py:592
  60.0 13.2 %project.1.q_ref.k_ref.v_ref = bf16[2048,2304]{1,0:T(8,128)(2,1)} custom-call(bf16[2048,768]{1,0:T(8,128)(2,1)} %x_ref.5, f32[1,768]{1,0:T(1,128)} %reshape.152.gain_ref, f32[1,768]{1,0:T(1,128)} %reshape.153.shift_ref, bf16[768,2304]{1,0:T(8,128)(2,1)} %all-gather.5.cloned.1.call-done.w_ref), custom_call_target="tpu_custom_call" | custom-call | tf_op jit(solution)/shard_map/project/pallas_call | solution.py:68
  73.1 56.8 %attend.1 = (bf16[2048,768]{1,0:T(8,128)(2,1)}, bf16[2,12,512,512]{3,2,1,0:T(8,128)(2,1)}, bf16[2,12,512,1024]{3,2,1,0:T(8,128)(2,1)}) custom-call(s32[2,2]{1,0:T(2,128)} %start_ref.3, s32[2,2]{1,0:T(2,128)} %length_ref.3, bf16[2048,2304]{1,0:T(8,128)(2,1)} %project.1.q_ref.k_ref.v_ref, bf16[2048,2304]{1,0:T(8,128)(2,1)} %project.1.q_ref.k_ref.v_ref, ...), custom_call_target="tpu_custom_call" | custom-call | tf_op jit(solution)/shard_map/attend/pallas_call | solution.py:185
  130.0 24.2 %all-gather.11.cloned.1.call-done.wd_hbm = bf16[3072,768]{1,0:T(8,128)(2,1)} async-done(((bf16[192,768]{1,0:T(8,128)(2,1)}), bf16[3072,768]{1,0:T(8,128)(2,1)}) %all-gather.11.cloned.1.call-update) | async-done | bytes 4718608 | tf_op jit(solution)/shard_map/all_gather | solution.py:592
  154.2 53.9 %all-gather.9.cloned.1.call-done.wu_hbm = bf16[768,3072]{1,0:T(8,128)(2,1)} async-done(((bf16[48,3072]{1,0:T(8,128)(2,1)}), bf16[768,3072]{1,0:T(8,128)(2,1)}) %all-gather.9.cloned.1.call-update) | async-done | bytes 4718608 | tf_op jit(solution)/shard_map/all_gather | solution.py:592
  208.2 102.0 %feed.1 = (bf16[2048,768]{1,0:T(8,128)(2,1)}, f32[2048,768]{1,0:T(8,128)}, bf16[2048,768]{1,0:T(8,128)(2,1)}, f32[7,1,768]{2,1,0:T(1,128)}, bf16[768,768]{1,0:T(...) custom-call(bf16[2048,768]{1,0:T(8,128)(2,1)} %x_ref.5, ...), custom_call_target="tpu_custom_call" | custom-call | tf_op jit(solution)/shard_map/feed/pallas_call | solution.py:462
  310.2 0.0 reduce-scatter.5.cloned.1.call-start
  310.3 65.5 %attend_back.1 = (bf16[2048,768]{1,0:T(8,128)(2,1)}, bf16[2048,768]{1,0:T(8,128)(2,1)}, bf16[2048,768]{1,0:T(8,128)(2,1)}) custom-call(s32[2,2]{1,0:T(2,128)} %start_ref.3, s32[2,2]{1,0:T(2,128)} %length_ref.3, bf16[2048,2304]{1,0:T(8,128)(2,1)} %project.1.q_ref.k_ref.v_ref, bf16[2048,2304]{1,0:T(8,128)(2,1)} %project.1.q_ref.k_ref.v_ref, ...), custom_call_target="tpu_custom_call" | custom-call | tf_op jit(solution)/shard_map/attend_back/pallas_call | solution.py:294
  375.8 26.9 %input_back.1 = (f32[2048,768]{1,0:T(8,128)}, f32[2,1,768]{2,1,0:T(1,128)}, bf16[768,2304]{1,0:T(8,128)(2,1)}) custom-call(bf16[2048,768]{1,0:T(8,128)(2,1)} %x_ref.5, f32[2048,768]{1,0:T(8,128)} %get-tuple-element.30.gmid_ref, bf16[2048,768]{1,0:T(8,128)(2,1)} %get-tuple-element.34.gq_ref, bf16[2048,768]{1,0:T(8,128)(2,1)} %get-tuple-element.35.gk_ref, ...), custom_call_target="tpu_custom_call" | custom-call | tf_op jit(solution)/shard_map/input_back/pallas_call | solution.py:571
  402.7 0.0 reduce-scatter.11.cloned.1.call-start
  402.8 0.7 reduce-scatter.11.cloned.1.call-update
  403.6 0.7 reduce-scatter.9.cloned.1.call-update
  404.3 0.0 all-reduce.6.cloned.1.call-start
  404.3 65.1 %reduce-scatter.5.cloned.1.call-done = bf16[48,2304]{1,0:T(8,128)(2,1)} async-done(((bf16[768,2304]{1,0:T(8,128)(2,1)}), bf16[48,2304]{1,0:T(8,128)(2,1)}) %reduce-scatter.5.cloned.1.call-update) | async-done | bytes 221200 | tf_op jit(solution)/shard_map/reduce_scatter | solution.py:641
  469.4 78.4 %reduce-scatter.11.cloned.1.call-done = bf16[192,768]{1,0:T(8,128)(2,1)} async-done(((bf16[3072,768]{1,0:T(8,128)(2,1)}), bf16[192,768]{1,0:T(8,128)(2,1)}) %reduce-scatter.11.cloned.1.call-update) | async-done | bytes 294928 | tf_op jit(solution)/shard_map/reduce_scatter | solution.py:641
  547.8 79.0 %reduce-scatter.9.cloned.1.call-done = bf16[48,3072]{1,0:T(8,128)(2,1)} async-done(((bf16[768,3072]{1,0:T(8,128)(2,1)}), bf16[48,3072]{1,0:T(8,128)(2,1)}) %reduce-scatter.9.cloned.1.call-update) | async-done | bytes 294928 | tf_op jit(solution)/shard_map/reduce_scatter | solution.py:641
  626.8 0.6 dynamic-slice
  628.1 0.1 reshape_squeeze.15
  628.2 0.1 reshape_squeeze.16
  628.4 0.1 reshape_squeeze.17
  628.5 0.1 reshape_squeeze.18
  628.5 0.1 reshape_squeeze.19
  628.6 0.1 slice_reduce_fusion
  628.7 0.1 reshape_reshape.3
  628.8 0.1 concatenate.9
  628.9 58.1 %all-reduce.2 = bf16[128,128]{1,0:T(8,128)(2,1)S(1)} all-reduce(bf16[128,128]{1,0:T(8,128)(2,1)S(1)} %reshape.149), channel_id=6, replica_groups=mesh['fsdp'=16,'rep'=2] {'fsdp'}, use_global_device_ids=true, to_apply=%region_8.9.clone | all-reduce | flops 16384 | bytes 65536
  687.0 4.9 psum.39
  691.9 0.6 slice.82
  692.6 0.6 fusion
  693.2 1.8 convert_element_type.72
  695.0 1.8 convert_element_type.73
  696.8 1.7 convert_element_type.70
  698.5 1.6 convert_element_type.71
  (26 shorter events, 0.4 us)
Async XLA Ops:
  7.2 52.8 %all-gather.5.cloned.1.call-start = ((), (), s32[]{:S(2)}) async-start(), calls=%async_computation.4 | async-start | bytes 3760128 | tf_op jit(solution)/shard_map/all_gather | solution.py:592
  7.9 122.1 %all-gather.7.cloned.1.call-start = ((), (), s32[]{:S(2)}) async-start(), calls=%async_computation.5 | async-start | bytes 1253376 | tf_op jit(solution)/shard_map/all_gather | solution.py:592
  8.7 145.5 %all-gather.11.cloned.1.call-start = ((), (), s32[]{:S(2)}) async-start(), calls=%async_computation.7 | async-start | bytes 5013504 | tf_op jit(solution)/shard_map/all_gather | solution.py:592
  9.4 198.8 %all-gather.9.cloned.1.call-start = ((), (), s32[]{:S(2)}) async-start(), calls=%async_computation.6 | async-start | bytes 5013504 | tf_op jit(solution)/shard_map/all_gather | solution.py:592
  10.0 394.4 %reduce-scatter.7.cloned.1.call-start = ((), (), s32[]{:S(2)}) async-start(), calls=%async_computation.9 | async-start | bytes 1253376 | tf_op jit(solution)/shard_map/reduce_scatter | solution.py:641
  310.2 159.2 %reduce-scatter.5.cloned.1.call-start = ((), (), s32[]{:S(2)}) async-start(), calls=%async_computation.8 | async-start | bytes 3760128 | tf_op jit(solution)/shard_map/reduce_scatter | solution.py:641
  402.7 145.1 %reduce-scatter.11.cloned.1.call-start = ((), (), s32[]{:S(2)}) async-start(), calls=%async_computation.11 | async-start | bytes 5013504 | tf_op jit(solution)/shard_map/reduce_scatter | solution.py:641
  403.5 223.3 %copy-start.2 = (u32[32]{0:T(128)S(1)}, u32[32]{0:T(128)}, u32[]{:S(2)}) copy-start(u32[32]{0:T(128)} %constant.11) | copy-start | bytes 388
  403.5 224.6 %copy-start.1 = (f32[2,1,768]{2,1,0:T(1,128)S(1)}, f32[2,1,768]{2,1,0:T(1,128)}, u32[]{:S(2)}) copy-start(f32[2,1,768]{2,1,0:T(1,128)} %get-tuple-element.42) | copy-start | bytes 18436
  403.5 224.8 %copy-start = (f32[7,1,768]{2,1,0:T(1,128)S(1)}, f32[7,1,768]{2,1,0:T(1,128)}, u32[]{:S(2)}) copy-start(f32[7,1,768]{2,1,0:T(1,128)} %get-tuple-element.43) | copy-start | bytes 64516
  403.5 223.3 %reduce-scatter.9.cloned.1.call-start = ((), (), s32[]{:S(2)}) async-start(), calls=%async_computation.10 | async-start | bytes 5013504 | tf_op jit(solution)/shard_map/reduce_scatter | solution.py:641
  404.3 288.9 %all-reduce.6.cloned.1.call-start = ((), (), s32[]{:S(2)}) async-start(), calls=%async_computation.12 | async-start | bytes 1769472 | tf_op jit(solution)/shard_map/psum | solution.py:644
Sparse Core Ops, SparseCore 0:
  10.3 49.6 all-gather.4
  62.2 37.3 all-gather.6
  101.9 52.2 all-gather.10
  156.3 51.7 all-gather.8
  310.4 56.6 reduce-scatter.6
  402.9 66.5 reduce-scatter.4
  473.3 74.4 reduce-scatter.10
  552.2 74.5 reduce-scatter.8
  629.3 36.0 all-reduce.5

commit v2 on v1

--- a/solution.py
+++ b/solution.py
@@ -13,6 +13,8 @@
 MASKED_VALUE = -1e30
 EPSILON = 1e-05
 SCALE = HEAD_DIM**-0.5
+GAIN1, SHIFT1, GAIN2, SHIFT2, DOWN_BIAS = (4, 5, 6, 7, 8)
+LINES = 16
 GELU_IN = 0.7978845608028654
 GELU_CUBE = 0.044715
 VMEM_LIMIT = 60 * 1024 * 1024
@@ -55,30 +57,317 @@
     return pltpu.CompilerParams(dimension_semantics=semantics, vmem_limit_bytes=VMEM_LIMIT)
 
 
-def project_kernel(x_ref, gain_ref, shift_ref, w_ref, o_ref):
-    normed, _ = normalize(x_ref[...].astype(F32))
-    normed = (normed * gain_ref[...] + shift_ref[...]).astype(BF16)
-    o_ref[...] = dot(normed, w_ref[...]).astype(BF16)
-
-
-def project(tokens, gain, shift, weight):
-    count, width = tokens.shape
-    columns = weight.shape[1]
-    block = 512
+def comm_params(number, *semantics):
+    return pltpu.CompilerParams(
+        dimension_semantics=semantics,
+        vmem_limit_bytes=VMEM_LIMIT,
+        collective_id=number,
+        has_side_effects=True,
+    )
+
+
+MESH = pl.DeviceIdType.MESH
+LEVELS = 4
+CORES = 2
+
+
+class Place:
+    def __init__(self, count, copies):
+        self.count, self.copies = (count, copies)
+        self.columns = count // (LEVELS * CORES)
+        self.index = lax.axis_index("fsdp")
+        self.rep = lax.axis_index("rep")
+        self.core = lax.rem(self.index, CORES)
+        chip = lax.div(self.index, CORES)
+        self.column = lax.rem(chip, self.columns)
+        self.level = lax.div(chip, self.columns)
+        self.half = lax.rem(self.rep, 2)
+
+    def block(self, up=0, across=0, other=0):
+        level = lax.rem(self.level + (up + LEVELS), LEVELS)
+        column = lax.rem(self.column + (across + self.columns), self.columns)
+        core = lax.rem(self.core + other, CORES)
+        return (level * self.columns + column) * CORES + core
+
+    def device(self, up=0, across=0, other=0, copy=0):
+        return (self.block(up, across, other), lax.rem(self.rep + copy, self.copies))
+
+    def twin(self):
+        return (self.index, self.rep + 1 - 2 * self.half)
+
+    def meet(self, twin=False, copies=False):
+        others = [self.device(up=up) for up in range(1, LEVELS)]
+        others += [self.device(across=across) for across in range(1, self.columns)]
+        others += [self.device(other=1)]
+        if twin:
+            others += [self.twin()]
+        if copies:
+            others += [self.device(copy=copy) for copy in range(1, self.copies)]
+        barrier = pltpu.get_barrier_semaphore()
+        for other in others:
+            pl.semaphore_signal(barrier, inc=1, device_id=other, device_id_type=MESH)
+        pl.semaphore_wait(barrier, len(others))
+
+
+def send(source, target, sems, slot, device):
+    return pltpu.make_async_remote_copy(
+        src_ref=source,
+        dst_ref=target,
+        send_sem=sems.at[2 * slot],
+        recv_sem=sems.at[2 * slot + 1],
+        device_id=device,
+        device_id_type=MESH,
+    )
+
+
+def gather_sems(count):
+    return 2 * (LEVELS - 1 + 3 * count // CORES) + 1
+
+
+class Gather:
+    def __init__(self, place, source, target, rows, shared, sems):
+        self.place, self.source, self.target = (place, source, target)
+        self.sems, self.shared = (sems, shared)
+        if shared:
+            third = rows // 3
+            half = place.half
+            self.part = pl.ds(pl.multiple_of(half * third, third), 2 * third)
+            self.give = pl.ds(pl.multiple_of(half * (2 * third), third), third)
+        else:
+            self.part = pl.ds(0, rows)
+
+    def held(self, up, across):
+        if up == 0 and across == 0:
+            return self.source
+        return self.target(self.place.block(-up, -across))
+
+    def slot(self, phase, up, across):
+        area = self.place.count // CORES
+        return LEVELS - 1 + phase * area + across * LEVELS + up
+
+    def level_copies(self):
+        target = self.target(self.place.block()).at[self.part, :]
+        source = self.source.at[self.part, :]
+        return [
+            send(source, target, self.sems, up - 1, self.place.device(up=up))
+            for up in range(1, LEVELS)
+        ]
+
+    def column_copies(self, ups):
+        place = self.place
+        return [
+            send(
+                self.held(up, 0).at[self.part, :],
+                self.target(place.block(-up)).at[self.part, :],
+                self.sems,
+                self.slot(0, up, across),
+                place.device(across=across),
+            )
+            for up in ups
+            for across in range(1, place.columns)
+        ]
+
+    def twin_copies(self, acrosses):
+        if not self.shared:
+            return []
+        place = self.place
+        return [
+            send(
+                self.held(up, across).at[self.give, :],
+                self.target(place.block(-up, -across)).at[self.give, :],
+                self.sems,
+                self.slot(1, up, across),
+                place.twin(),
+            )
+            for across in acrosses
+            for up in range(LEVELS)
+            if up or across
+        ]
+
+    def core_copies(self, first):
+        place = self.place
+        return [
+            send(
+                self.held(up, across),
+                self.target(place.block(-up, -across)),
+                self.sems,
+                self.slot(2, up, across),
+                place.device(other=1),
+            )
+            for across in range(place.columns)
+            for up in range(LEVELS)
+            if (up == 0 and across == 0) == first
+        ]
+
+    def own(self):
+        last = gather_sems(self.place.count) - 1
+        return pltpu.make_async_copy(
+            self.source, self.target(self.place.block()), self.sems.at[last]
+        )
+
+    def start(self):
+        for copy in self.level_copies() + self.column_copies([0]) + self.core_copies(True):
+            copy.start()
+        self.own().start()
+
+    def after_levels(self):
+        for copy in self.level_copies():
+            copy.wait_recv()
+        for copy in self.column_copies(range(1, LEVELS)) + self.twin_copies([0]):
+            copy.start()
+
+    def after_columns(self):
+        for copy in self.column_copies(range(LEVELS)):
+            copy.wait_recv()
+        for copy in self.twin_copies(range(1, self.place.columns)):
+            copy.start()
+        if not self.shared:
+            self.to_cores()
+
+    def after_twins(self):
+        for copy in self.twin_copies(range(self.place.columns)):
+            copy.wait_recv()
+        if self.shared:
+            self.to_cores()
+
+    def to_cores(self):
+        for copy in self.core_copies(False):
+            copy.start()
+
+    def finish(self):
+        for copy in self.core_copies(True) + self.core_copies(False):
+            copy.wait_recv()
+        self.own().wait()
+
+    def drain(self):
+        columns = range(self.place.columns)
+        copies = self.level_copies() + self.column_copies(range(LEVELS))
+        copies += self.twin_copies(columns) + self.core_copies(True) + self.core_copies(False)
+        for copy in copies:
+            copy.wait_send()
+
+
+def project_kernel(
+    count,
+    copies,
+    x_ref,
+    w_hbm,
+    vec_hbm,
+    o_ref,
+    full_hbm,
+    vec_ref,
+    n1_ref,
+    w_ref,
+    all_ref,
+    sems,
+    load_sem,
+):
+    step = pl.program_id(0)
+    width = x_ref.shape[1]
+    rows = w_hbm.shape[0]
+    lines = vec_hbm.shape[0]
+    place = Place(count, copies)
+    pieces = [
+        Gather(
+            place,
+            vec_hbm,
+            lambda block: all_ref.at[pl.ds(pl.multiple_of(block * lines, lines), lines), :],
+            lines,
+            False,
+            sems.at[0],
+        )
+    ]
+    for which in range(3):
+        columns = pl.ds(which * width, width)
+
+        def target(block, columns=columns):
+            return full_hbm.at[pl.ds(pl.multiple_of(block * rows, rows), rows), columns]
+
+        pieces.append(
+            Gather(place, w_hbm.at[:, columns], target, rows, False, sems.at[1 + which])
+        )
+
+    def multiply(which):
+        pieces[1 + which].finish()
+        copy = pltpu.make_async_copy(
+            full_hbm.at[:, pl.ds(which * width, width)], w_ref, load_sem
+        )
+        copy.start()
+        copy.wait()
+        o_ref[...] = dot(n1_ref[...], w_ref[...]).astype(BF16)
+
+    @pl.when(step == 0)
+    def _():
+        place.meet()
+        for piece in pieces:
+            piece.start()
+        pieces[0].after_levels()
+        pieces[0].after_columns()
+        pieces[1].after_levels()
+        pieces[0].finish()
+        vectors = all_ref[0:lines, :].astype(F32)
+        for other in range(1, count):
+            vectors = vectors + all_ref[other * lines : (other + 1) * lines, :].astype(F32)
+        for line in range(lines):
+            vec_ref[line] = vectors[line : line + 1, :]
+        total = x_ref.shape[0]
+        gain, shift = (vec_ref[GAIN1], vec_ref[SHIFT1])
+        block = 256
+
+        def norm_rows(i, carry):
+            at = pl.ds(pl.multiple_of(i * block, block), block)
+            normed, _ = normalize(x_ref[at, :].astype(F32))
+            n1_ref[at, :] = (normed * gain + shift).astype(BF16)
+            return carry
+
+        lax.fori_loop(0, total // block, norm_rows, 0)
+        pieces[1].after_columns()
+        pieces[2].after_levels()
+        pieces[2].after_columns()
+        multiply(0)
+
+    @pl.when(step == 1)
+    def _():
+        pieces[3].after_levels()
+        pieces[3].after_columns()
+        multiply(1)
+
+    @pl.when(step == 2)
+    def _():
+        multiply(2)
+        for piece in pieces:
+            piece.drain()
+
+
+def project(tokens, weight, vectors, count, copies):
+    total, width = tokens.shape
+    rows, columns = weight.shape
+    lines = vectors.shape[0]
+    anywhere = pl.BlockSpec(memory_space=pl.ANY)
     return pl.pallas_call(
-        project_kernel,
-        out_shape=jax.ShapeDtypeStruct((count, columns), BF16),
-        grid=(count // block,),
-        in_specs=[
-            pl.BlockSpec((block, width), lambda i: (i, 0)),
-            pl.BlockSpec((1, width), lambda i: (0, 0)),
-            pl.BlockSpec((1, width), lambda i: (0, 0)),
-            pl.BlockSpec((width, columns), lambda i: (0, 0)),
+        functools.partial(project_kernel, count, copies),
+        out_shape=[
+            jax.ShapeDtypeStruct((total, columns), BF16),
+            jax.ShapeDtypeStruct((rows * count, columns), BF16),
+            jax.ShapeDtypeStruct((lines, 1, width), F32),
         ],
-        out_specs=pl.BlockSpec((block, columns), lambda i: (i, 0)),
-        compiler_params=params("arbitrary"),
+        grid=(3,),
+        in_specs=[pl.BlockSpec((total, width), lambda i: (0, 0)), anywhere, anywhere],
+        out_specs=[
+            pl.BlockSpec((total, width), lambda i: (0, i)),
+            anywhere,
+            pl.BlockSpec((lines, 1, width), lambda i: (0, 0, 0)),
+        ],
+        scratch_shapes=[
+            pltpu.VMEM((total, width), BF16),
+            pltpu.VMEM((width, width), BF16),
+            pltpu.VMEM((count * lines, width), BF16),
+            pltpu.SemaphoreType.DMA((4, gather_sems(count))),
+            pltpu.SemaphoreType.DMA,
+        ],
+        compiler_params=comm_params(0, "arbitrary"),
         name="project",
-    )(tokens, gain, shift, weight)
+    )(tokens, weight, vectors)
 
 
 def label_of(position, start_ref, length_ref, seq, pieces):
@@ -450,14 +739,17 @@
         copies[-1].wait()
 
 
-def feed(tokens, mixed, cotangent, gain, shift, up_bias, down_bias, wo, wu, wd):
+def vector_line(row):
+    return lambda width: pl.BlockSpec((None, 1, width), lambda *_: (row, 0, 0))
+
+
+def feed(tokens, mixed, cotangent, vectors, wo, wu, wd):
     count, width = tokens.shape
     hidden = wu.shape[1]
     block = 512
     chunk = width
     chunks = hidden // chunk
     rows = pl.BlockSpec((block, width), lambda i: (i, 0))
-    line = pl.BlockSpec((1, width), lambda i: (0, 0))
     anywhere = pl.BlockSpec(memory_space=pl.ANY)
     return pl.pallas_call(
         functools.partial(feed_kernel, chunk),
@@ -475,10 +767,10 @@
             rows,
             rows,
             rows,
-            line,
-            line,
+            vector_line(GAIN2)(width),
+            vector_line(SHIFT2)(width),
             pl.BlockSpec((chunks, 1, chunk), lambda i: (0, 0, 0)),
-            line,
+            vector_line(DOWN_BIAS)(width),
             anywhere,
             anywhere,
             anywhere,
@@ -513,10 +805,10 @@
         tokens,
         mixed,
         cotangent,
-        gain,
-        shift,
-        up_bias.reshape(chunks, 1, chunk),
-        down_bias,
+        vectors,
+        vectors,
+        vectors,
+        vectors,
         wo,
         wu,
         wd,
@@ -563,11 +855,10 @@
             gw_ref[:, which * width : (which + 1) * width] = acc_ref[which].astype(BF16)
 
 
-def input_back(tokens, grad_middle, grads, gain, shift, weight):
+def input_back(tokens, grad_middle, grads, vectors, weight):
     count, width = tokens.shape
     block = 512
     rows = pl.BlockSpec((block, width), lambda i: (i, 0))
-    line = pl.BlockSpec((1, width), lambda i: (0, 0))
     return pl.pallas_call(
         input_kernel,
         out_shape=[
@@ -576,7 +867,9 @@
             jax.ShapeDtypeStruct(weight.shape, BF16),
         ],
         grid=(count // block,),
-        in_specs=[rows] * 5 + [line, line, pl.BlockSpec(weight.shape, lambda i: (0, 0))],
+        in_specs=[rows] * 5
+        + [vector_line(GAIN1)(width), vector_line(SHIFT1)(width)]
+        + [pl.BlockSpec(weight.shape, lambda i: (0, 0))],
         out_specs=[
             rows,
             pl.BlockSpec((2, 1, width), lambda i: (0, 0, 0)),
@@ -585,7 +878,7 @@
         scratch_shapes=[pltpu.VMEM((3, width, width), F32)],
         compiler_params=params("arbitrary"),
         name="input_back",
-    )(tokens, grad_middle, *grads, gain, shift, weight)
+    )(tokens, grad_middle, *grads, vectors, vectors, weight)
 
 
 def gather(value):
@@ -609,32 +902,30 @@
     cotangent,
 ):
     width = tokens.shape[1]
-    vectors = (first_gain, first_shift, second_gain, second_shift, up_bias, down_bias)
-    sizes = [v.shape[0] for v in vectors]
-    total = sum(sizes)
-    padded = -(-total // 1024) * 1024
-    flat = jnp.pad(jnp.concatenate(vectors), (0, padded - total)).reshape(1, 8, padded // 8)
-    flat = gather(flat).reshape(-1, padded)
-    vectors, at = ([], 0)
-    for size in sizes:
-        vectors.append(flat[:, at : at + size].reshape(1, -1))
-        at += size
-    gain1, shift1, gain2, shift2, up_bias, down_bias = (v.astype(F32) for v in vectors)
-
-    wqkv = gather(query_key_value)
+    devices, copies = (lax.axis_size("fsdp"), lax.axis_size("rep"))
+    index = lax.axis_index("fsdp")
+
+    def placed(vector):
+        flat = jnp.zeros((devices * vector.shape[0],), BF16)
+        flat = lax.dynamic_update_slice(flat, vector, (index * vector.shape[0],))
+        return flat.reshape(-1, width)
+
+    own = [up_bias, first_gain, first_shift, second_gain, second_shift, down_bias]
+    own = jnp.concatenate([placed(vector) for vector in own], axis=0)
+    own = jnp.pad(own, ((0, LINES - own.shape[0]), (0, 0)))
+
     wo = gather(output_weight)
     wu = gather(up_weight)
     wd = gather(down_weight)
 
-    projected = project(tokens, gain1, shift1, wqkv)
+    projected, wqkv, vectors = project(tokens, query_key_value, own, devices, copies)
     mixed, attention = attend(projected, piece_start, piece_length)
     block_output, grad_middle, grad_mixed, small2, gwo, gwu, gwd = feed(
-        tokens, mixed, cotangent, gain2, shift2, up_bias, down_bias, wo, wu, wd
+        tokens, mixed, cotangent, vectors, wo, wu, wd
     )
     grads = attend_back(projected, piece_start, piece_length, grad_mixed, mixed, attention)
-    grad_tokens, small1, gwqkv = input_back(tokens, grad_middle, grads, gain1, shift1, wqkv)
-
-    devices = lax.axis_size("fsdp")
+    grad_tokens, small1, gwqkv = input_back(tokens, grad_middle, grads, vectors, wqkv)
+
     small = jnp.concatenate([small1.reshape(-1, width), small2.reshape(-1, width)], axis=0)
 
     def scatter(value):
@@ -644,8 +935,10 @@
         return lax.psum(value, "rep").astype(F32)
 
     small = small.astype(BF16)
-    hidden = up_bias.shape[1]
     order = [small[0], small[1], small[2], small[3], small[5:].reshape(-1), small[4]]
+    sizes = [v.size // devices for v in order]
+    total = sum(sizes)
+    padded = -(-total // 1024) * 1024
     packed = jnp.concatenate([v.reshape(devices, -1) for v in order], axis=1)
     packed = jnp.pad(packed, ((0, 0), (0, padded - total))).reshape(devices * 8, padded // 8)
     packed = across(scatter(packed)).reshape(-1)

time: 714 us -> 670 us (0.938)
  waiting for transfers between devices: 323 us -> 260 us
  Pallas kernels: 264 us -> 309 us
  blocking collectives: 86.3 us -> 63 us
    all_gather x4 -> x3, waiting for transfers between devices: 96.6 us -> 34.1 us  [gather(): return lax.all_gather(value, 'fsdp', axis=0, tiled=True)]
    pallas_call x1, Pallas kernels: 13.2 us -> 57.1 us  [project(): pl.pallas_call(functools.partial(project_kernel, count, copies), out_shap...]
    all_gather x1 -> x0, blocking collectives: 23.2 us -> none  [gather(): return lax.all_gather(value, 'fsdp', axis=0, tiled=True)]
  transfers between devices with their start and end apart: 9 -> 8, of which waited for: 6 -> 4; matrix products, arithmetic and copies ran while one was open for 2% -> 1% of each run, Pallas kernels for 23% -> 31%
where the time goes in v2:
time: 670 us; the launch traced here: 662 us
  Pallas kernels  309 us (46%)
  waiting for transfers between devices  260 us (39%)
  blocking collectives  63 us (9%)
  between operations  15.2 us (2%)
  local copies, waits for them, and re-layouts  8.09 us (1%)
  other arithmetic  6.93 us (1%)
    reduce_scatter x4, waiting for transfers between devices, scatter(): return lax.psum_scatter(value, 'fsdp', scatter_dimension=0, tiled=True)  222 us
    pallas_call x1, Pallas kernels, feed(): pl.pallas_call(functools.partial(feed_kernel, chunk), out_shape=[jax.Shap...  102 us
    pallas_call x1, Pallas kernels, attend_back(): pl.pallas_call(functools.partial(attend_back_kernel, slot, pieces), out_s...  65.4 us
    unnamed x1, blocking collectives  58 us
    pallas_call x1, Pallas kernels, project(): pl.pallas_call(functools.partial(project_kernel, count, copies), out_shap...  57.1 us
    pallas_call x1, Pallas kernels, attend(): pl.pallas_call(functools.partial(attend_kernel, slot, pieces), out_shape=...  57.1 us
    all_gather x3, waiting for transfers between devices, gather(): return lax.all_gather(value, 'fsdp', axis=0, tiled=True)  34.1 us
    pallas_call x1, Pallas kernels, input_back(): pl.pallas_call(input_kernel, out_shape=[jax.ShapeDtypeStruct((count, widt...  26.9 us
  transfers between devices with their start and end apart: 8, of which 4 were waited for; matrix products, arithmetic and copies ran while one was open for 1% of the time, Pallas kernels for 31%

profile of v2, /device:TPU:0, one launch (start us, length us, event | category | flops | bytes accessed | tf_op | source)
XLA Modules:
  0.0 662.0 jit_solution(18155833112148475614)
XLA Ops:
  7.2 0.0 all-gather.4.cloned.1.call-start
  7.2 0.7 all-gather.4.cloned.1.call-update
  7.9 0.0 all-gather.6.cloned.1.call-start
  8.0 0.7 all-gather.6.cloned.1.call-update
  8.7 0.0 all-gather.8.cloned.1.call-start
  8.7 0.7 all-gather.8.cloned.1.call-update
  9.4 0.0 reduce-scatter.7.cloned.1.call-start
  9.5 0.9 dynamic_update_slice.23
  10.3 0.8 dynamic_update_slice.24
  11.1 0.8 dynamic_update_slice.25
  11.9 0.8 dynamic_update_slice.26
  12.7 0.8 dynamic_update_slice.27
  13.6 0.8 dynamic_update_slice.28
  14.3 0.1 concatenate.8
  14.4 0.6 pad.8.vec_hbm
  15.0 57.1 %project.1 = (bf16[2048,2304]{1,0:T(8,128)(2,1)}, bf16[768,2304]{1,0:T(8,128)(2,1)}, f32[16,1,768]{2,1,0:T(1,128)}) custom-call(bf16[2048,768]{1,0:T(8,128)(2,1)} %x_ref.5, bf16[48,2304]{1,0:T(8,128)(2,1)} %w_hbm.1, bf16[16,768]{1,0:T(8,128)(2,1)} %pad.8.vec_hbm), custom_call_target="tpu_custom_call" | custom-call | tf_op jit(solution)/shard_map/project/pallas_call | solution.py:347
  72.1 57.1 %attend.1 = (bf16[2048,768]{1,0:T(8,128)(2,1)}, bf16[2,12,512,512]{3,2,1,0:T(8,128)(2,1)}, bf16[2,12,512,1024]{3,2,1,0:T(8,128)(2,1)}) custom-call(s32[2,2]{1,0:T(2,128)} %start_ref.3, s32[2,2]{1,0:T(2,128)} %length_ref.3, bf16[2048,2304]{1,0:T(8,128)(2,1)} %get-tuple-element.31.q_ref.k_ref.v_ref, bf16[2048,2304]{1,0:T(8,128)(2,1)} %get-tuple-element.31.q_ref.k_ref.v_ref, ...), custom_call_target="tpu_custom_call" | custom-call | tf_op jit(solution)/shard_map/attend/pallas_call | solution.py:474
  129.2 34.1 %all-gather.8.cloned.1.call-done.wd_hbm = bf16[3072,768]{1,0:T(8,128)(2,1)} async-done(((bf16[192,768]{1,0:T(8,128)(2,1)}), bf16[3072,768]{1,0:T(8,128)(2,1)}) %all-gather.8.cloned.1.call-update) | async-done | bytes 4718608 | tf_op jit(solution)/shard_map/all_gather | solution.py:885
  163.2 102.1 %feed.1 = (bf16[2048,768]{1,0:T(8,128)(2,1)}, f32[2048,768]{1,0:T(8,128)}, bf16[2048,768]{1,0:T(8,128)(2,1)}, f32[7,1,768]{2,1,0:T(1,128)}, bf16[768,768]{1,0:T(...) custom-call(bf16[2048,768]{1,0:T(8,128)(2,1)} %x_ref.5, ...), custom_call_target="tpu_custom_call" | custom-call | tf_op jit(solution)/shard_map/feed/pallas_call | solution.py:754
  265.4 0.0 reduce-scatter.5.cloned.1.call-start
  265.5 65.4 %attend_back.1 = (bf16[2048,768]{1,0:T(8,128)(2,1)}, bf16[2048,768]{1,0:T(8,128)(2,1)}, bf16[2048,768]{1,0:T(8,128)(2,1)}) custom-call(s32[2,2]{1,0:T(2,128)} %start_ref.3, s32[2,2]{1,0:T(2,128)} %length_ref.3, bf16[2048,2304]{1,0:T(8,128)(2,1)} %get-tuple-element.31.q_ref.k_ref.v_ref, bf16[2048,2304]{1,0:T(8,128)(2,1)} %get-tuple-element.31.q_ref.k_ref.v_ref, ...), custom_call_target="tpu_custom_call" | custom-call | tf_op jit(solution)/shard_map/attend_back/pallas_call | solution.py:583
  330.9 26.9 %input_back.1 = (f32[2048,768]{1,0:T(8,128)}, f32[2,1,768]{2,1,0:T(1,128)}, bf16[768,2304]{1,0:T(8,128)(2,1)}) custom-call(bf16[2048,768]{1,0:T(8,128)(2,1)} %x_ref.5, f32[2048,768]{1,0:T(8,128)} %get-tuple-element.35.gmid_ref, bf16[2048,768]{1,0:T(8,128)(2,1)} %get-tuple-element.39.gq_ref, bf16[2048,768]{1,0:T(8,128)(2,1)} %get-tuple-element.40.gk_ref, ...), custom_call_target="tpu_custom_call" | custom-call | tf_op jit(solution)/shard_map/input_back/pallas_call | solution.py:862
  357.8 0.0 reduce-scatter.5.cloned.1.call-update
  357.8 0.0 reduce-scatter.11.cloned.1.call-start
  357.8 0.5 reduce-scatter.11.cloned.1.call-update
  358.4 0.0 reduce-scatter.9.cloned.1.call-start
  358.4 0.7 reduce-scatter.9.cloned.1.call-update
  359.1 0.0 all-reduce.6.cloned.1.call-start
  359.2 0.0 reduce-scatter.7.cloned.1.call-done
  359.2 65.3 %reduce-scatter.5.cloned.1.call-done = bf16[48,2304]{1,0:T(8,128)(2,1)} async-done(((bf16[768,2304]{1,0:T(8,128)(2,1)}), bf16[48,2304]{1,0:T(8,128)(2,1)}) %reduce-scatter.5.cloned.1.call-update) | async-done | bytes 221200 | tf_op jit(solution)/shard_map/reduce_scatter | solution.py:932
  424.5 78.2 %reduce-scatter.11.cloned.1.call-done = bf16[192,768]{1,0:T(8,128)(2,1)} async-done(((bf16[3072,768]{1,0:T(8,128)(2,1)}), bf16[192,768]{1,0:T(8,128)(2,1)}) %reduce-scatter.11.cloned.1.call-update) | async-done | bytes 294928 | tf_op jit(solution)/shard_map/reduce_scatter | solution.py:932
  502.7 79.0 %reduce-scatter.9.cloned.1.call-done = bf16[48,3072]{1,0:T(8,128)(2,1)} async-done(((bf16[768,3072]{1,0:T(8,128)(2,1)}), bf16[48,3072]{1,0:T(8,128)(2,1)}) %reduce-scatter.9.cloned.1.call-update) | async-done | bytes 294928 | tf_op jit(solution)/shard_map/reduce_scatter | solution.py:932
  581.7 0.6 dynamic-slice
  583.0 0.1 reshape_squeeze.15
  583.1 0.1 reshape_squeeze.16
  583.3 0.1 reshape_reshape.3
  583.4 0.1 reshape_squeeze.17
  583.5 0.1 reshape_squeeze.18
  583.6 0.1 reshape_squeeze.19
  583.6 0.1 concatenate.9
  583.8 58.0 %all-reduce.2 = bf16[128,128]{1,0:T(8,128)(2,1)S(1)} all-reduce(bf16[128,128]{1,0:T(8,128)(2,1)S(1)} %reshape.86), channel_id=6, replica_groups=mesh['fsdp'=16,'rep'=2] {'fsdp'}, use_global_device_ids=true, to_apply=%region_8.9.clone | all-reduce | flops 16384 | bytes 65536
  641.8 4.9 psum.39
  646.8 0.6 slice.58
  647.4 0.6 fusion
  648.0 1.8 convert_element_type.20
  649.8 1.8 convert_element_type.21
  651.6 1.7 convert_element_type.18
  653.3 1.6 convert_element_type.19
  (26 shorter events, 0.3 us)
Async XLA Ops:
  7.2 122.0 %all-gather.4.cloned.1.call-start = ((), (), s32[]{:S(2)}) async-start(), calls=%async_computation.4 | async-start | bytes 1253376 | tf_op jit(solution)/shard_map/all_gather | solution.py:885
  7.9 121.3 %all-gather.6.cloned.1.call-start = ((), (), s32[]{:S(2)}) async-start(), calls=%async_computation.5 | async-start | bytes 5013504 | tf_op jit(solution)/shard_map/all_gather | solution.py:885
  8.7 154.6 %all-gather.8.cloned.1.call-start = ((), (), s32[]{:S(2)}) async-start(), calls=%async_computation.6 | async-start | bytes 5013504 | tf_op jit(solution)/shard_map/all_gather | solution.py:885
  9.4 349.8 %reduce-scatter.7.cloned.1.call-start = ((), (), s32[]{:S(2)}) async-start(), calls=%async_computation.8 | async-start | bytes 1253376 | tf_op jit(solution)/shard_map/reduce_scatter | solution.py:932
  265.4 159.1 %reduce-scatter.5.cloned.1.call-start = ((), (), s32[]{:S(2)}) async-start(), calls=%async_computation.7 | async-start | bytes 3760128 | tf_op jit(solution)/shard_map/reduce_scatter | solution.py:932
  357.8 144.9 %reduce-scatter.11.cloned.1.call-start = ((), (), s32[]{:S(2)}) async-start(), calls=%async_computation.10 | async-start | bytes 5013504 | tf_op jit(solution)/shard_map/reduce_scatter | solution.py:932
  358.4 223.3 %copy-start.2 = (u32[32]{0:T(128)S(1)}, u32[32]{0:T(128)}, u32[]{:S(2)}) copy-start(u32[32]{0:T(128)} %constant.33) | copy-start | bytes 388
  358.4 224.6 %copy-start.1 = (f32[2,1,768]{2,1,0:T(1,128)S(1)}, f32[2,1,768]{2,1,0:T(1,128)}, u32[]{:S(2)}) copy-start(f32[2,1,768]{2,1,0:T(1,128)} %get-tuple-element.48) | copy-start | bytes 18436
  358.4 224.8 %copy-start = (f32[7,1,768]{2,1,0:T(1,128)S(1)}, f32[7,1,768]{2,1,0:T(1,128)}, u32[]{:S(2)}) copy-start(f32[7,1,768]{2,1,0:T(1,128)} %get-tuple-element.49) | copy-start | bytes 64516
  358.4 223.3 %reduce-scatter.9.cloned.1.call-start = ((), (), s32[]{:S(2)}) async-start(), calls=%async_computation.9 | async-start | bytes 5013504 | tf_op jit(solution)/shard_map/reduce_scatter | solution.py:932
  359.1 288.8 %all-reduce.6.cloned.1.call-start = ((), (), s32[]{:S(2)}) async-start(), calls=%async_computation.11 | async-start | bytes 1769472 | tf_op jit(solution)/shard_map/psum | solution.py:935
Sparse Core Ops, SparseCore 0:
  10.3 44.2 all-gather.3
  56.9 52.1 all-gather.5
  111.4 51.7 all-gather.7
  265.5 56.6 reduce-scatter.6
  357.9 66.5 reduce-scatter.4
  428.2 74.4 reduce-scatter.10
  507.0 74.5 reduce-scatter.8
  584.2 36.0 all-reduce.5

commit v3 on v2

--- a/solution.py
+++ b/solution.py
@@ -244,6 +244,229 @@
         copies = self.level_copies() + self.column_copies(range(LEVELS))
         copies += self.twin_copies(columns) + self.core_copies(True) + self.core_copies(False)
         for copy in copies:
+            copy.wait_send()
+
+
+def scatter_slots(count, copies):
+    area = count // CORES
+    return area + (area - LEVELS) + (LEVELS - 1) + (copies - 1)
+
+
+def scatter_scratch(count, copies, rows, columns):
+    across = count // (CORES * LEVELS)
+    return [
+        pltpu.VMEM((count, rows, columns), BF16),
+        pltpu.VMEM((across, LEVELS, rows, columns), BF16),
+        pltpu.VMEM((max(across - 1, 1), LEVELS, rows, columns), BF16),
+        pltpu.VMEM((LEVELS - 1, rows, columns), BF16),
+        pltpu.VMEM((copies, rows, columns), BF16),
+        pltpu.SemaphoreType.DMA((2 * scatter_slots(count, copies),)),
+    ]
+
+
+def add_low(left, right):
+    return (left.astype(F32) + right.astype(F32)).astype(BF16)
+
+
+class Scatter:
+    def __init__(self, place, refs, write):
+        self.place, self.write = (place, write)
+        self.held, self.from_core, self.from_column, self.from_level, self.parts, self.sems = refs
+        self.area = place.count // CORES
+
+    def core_copies(self):
+        place = self.place
+        return [
+            send(
+                self.held.at[place.block(up, across, 1)],
+                self.from_core.at[across, up],
+                self.sems,
+                across * LEVELS + up,
+                place.device(other=1),
+            )
+            for across in range(place.columns)
+            for up in range(LEVELS)
+        ]
+
+    def column_copies(self):
+        place = self.place
+        return [
+            send(
+                self.held.at[place.block(up, across)],
+                self.from_column.at[across - 1, up],
+                self.sems,
+                self.area + (across - 1) * LEVELS + up,
+                place.device(across=across),
+            )
+            for across in range(1, place.columns)
+            for up in range(LEVELS)
+        ]
+
+    def level_copies(self):
+        place = self.place
+        base = 2 * self.area - LEVELS
+        return [
+            send(
+                self.held.at[place.block(up)],
+                self.from_level.at[up - 1],
+                self.sems,
+                base + up - 1,
+                place.device(up=up),
+            )
+            for up in range(1, LEVELS)
+        ]
+
+    def rep_copies(self):
+        place = self.place
+        base = 2 * self.area - 1
+        mine = self.parts.at[place.rep]
+        return [
+            send(mine, mine, self.sems, base + copy - 1, place.device(copy=copy))
+            for copy in range(1, place.copies)
+        ]
+
+    def start(self):
+        for copy in self.core_copies():
+            copy.start()
+
+    def after_cores(self):
+        place = self.place
+        for copy in self.core_copies():
+            copy.wait_recv()
+
+        def add(i, carry):
+            across, up = (lax.div(i, LEVELS), lax.rem(i, LEVELS))
+            block = place.block(up, across)
+            self.held[block] = add_low(self.held[block], self.from_core[across, up])
+            return carry
+
+        lax.fori_loop(0, self.area, add, 0)
+        for copy in self.column_copies():
+            copy.start()
+
+    def after_columns(self):
+        place = self.place
+        for copy in self.column_copies():
+            copy.wait_recv()
+
+        def add(up, carry):
+            block = place.block(up)
+            total = self.held[block].astype(F32)
+            for across in range(place.columns - 1):
+                total = total + self.from_column[across, up].astype(F32)
+            self.held[block] = total.astype(BF16)
+            return carry
+
+        lax.fori_loop(0, LEVELS, add, 0)
+        for copy in self.level_copies():
+            copy.start()
+
+    def after_levels(self):
+        for copy in self.level_copies():
+            copy.wait_recv()
+        total = self.held[self.place.block()].astype(F32)
+        for level in range(LEVELS - 1):
+            total = total + self.from_level[level].astype(F32)
+        self.parts[self.place.rep] = total.astype(BF16)
+        for copy in self.rep_copies():
+            copy.start()
+
+    def after_copies(self):
+        for copy in self.rep_copies():
+            copy.wait_recv()
+        total = self.parts[0].astype(F32)
+        for rep in range(1, self.place.copies):
+            total = total + self.parts[rep].astype(F32)
+        self.write(total)
+
+    def drain(self):
+        copies = self.core_copies() + self.column_copies() + self.level_copies()
+        for copy in copies + self.rep_copies():
+            copy.wait_send()
+
+
+def reduce_scratch(count, copies, lines, width):
+    across = count // (CORES * LEVELS)
+    slots = 1 + (across - 1) + (LEVELS - 1) + (copies - 1)
+    return [
+        pltpu.VMEM((3, lines, 1, width), F32),
+        pltpu.VMEM((1 + across - 1 + LEVELS - 1, lines, 1, width), F32),
+        pltpu.VMEM((copies, lines, 1, width), F32),
+        pltpu.SemaphoreType.DMA((2 * slots,)),
+    ]
+
+
+class Reduce:
+    def __init__(self, place, refs, out):
+        self.place, self.out = (place, out)
+        self.sums, self.landed, self.parts, self.sems = refs
+
+    def group(self, phase):
+        place = self.place
+        if phase == 0:
+            targets = [place.device(other=1)]
+            first = 0
+        elif phase == 1:
+            targets = [place.device(across=across) for across in range(1, place.columns)]
+            first = 1
+        else:
+            targets = [place.device(up=up) for up in range(1, LEVELS)]
+            first = place.columns
+        return [
+            send(self.sums.at[phase], self.landed.at[first + i], self.sems, first + i, target)
+            for i, target in enumerate(targets)
+        ]
+
+    def rep_copies(self):
+        place = self.place
+        base = place.columns + LEVELS - 1
+        mine = self.parts.at[place.rep]
+        return [
+            send(mine, mine, self.sems, base + copy - 1, place.device(copy=copy))
+            for copy in range(1, place.copies)
+        ]
+
+    def start(self, value):
+        self.sums[0] = value
+        for copy in self.group(0):
+            copy.start()
+
+    def next(self, phase):
+        copies = self.group(phase)
+        for copy in copies:
+            copy.wait_recv()
+        first = (0, 1, self.place.columns)[phase]
+        total = self.sums[phase]
+        for i in range(len(copies)):
+            total = total + self.landed[first + i]
+        if phase < 2:
+            self.sums[phase + 1] = total
+            for copy in self.group(phase + 1):
+                copy.start()
+        else:
+            self.parts[self.place.rep] = total
+            for copy in self.rep_copies():
+                copy.start()
+
+    def after_cores(self):
+        self.next(0)
+
+    def after_columns(self):
+        self.next(1)
+
+    def after_levels(self):
+        self.next(2)
+
+    def after_copies(self):
+        for copy in self.rep_copies():
+            copy.wait_recv()
+        total = self.parts[0]
+        for rep in range(1, self.place.copies):
+            total = total + self.parts[rep]
+        self.out[...] = total
+
+    def drain(self):
+        for copy in self.group(0) + self.group(1) + self.group(2) + self.rep_copies():
             copy.wait_send()
 
 
@@ -407,13 +630,78 @@
     return (lane >= HEAD_DIM) if half else (lane < HEAD_DIM)
 
 
+def at_steps(step, table):
+    for when in sorted(set(table)):
+        @pl.when(step == when)
+        def _(when=when):
+            for action in table[when]:
+                action()
+
+
+def schedule(*entries):
+    table = {}
+    for when, action in entries:
+        table.setdefault(when, []).append(action)
+    return table
+
+
 def attend_kernel(
-    slot, pieces, start_ref, length_ref, q_ref, k_ref, v_ref, o_ref, *rest
+    slot,
+    pieces,
+    count,
+    copies,
+    start_ref,
+    length_ref,
+    q_ref,
+    k_ref,
+    v_ref,
+    wo_hbm,
+    wu_hbm,
+    wd_hbm,
+    o_ref,
+    *rest,
 ):
-    att_refs, (bias_ref, prefix_ref) = rest[:-2], rest[-2:]
+    att_refs = rest[:pieces]
+    full_o, full_u, full_d, bias_ref, prefix_ref, sems = rest[pieces:]
     seq = pl.program_id(0)
+    steps = pl.num_programs(0) * pl.num_programs(1)
+    step = seq * pl.num_programs(1) + pl.program_id(1)
     length = q_ref.shape[0]
     zero = jnp.zeros((), BF16)
+
+    place = Place(count, copies)
+    cuts = []
+    for shard, full, cut_rows, cut_columns in (
+        (wo_hbm, full_o, 1, 1),
+        (wu_hbm, full_u, 1, 2),
+        (wd_hbm, full_d, 2, 1),
+    ):
+        rows, columns = (shard.shape[0] // cut_rows, shard.shape[1] // cut_columns)
+        for i in range(cut_rows):
+            for j in range(cut_columns):
+                across = pl.ds(j * columns, columns)
+
+                def target(block, full=full, i=i, rows=rows, cut=cut_rows, across=across):
+                    first = pl.multiple_of(block * (rows * cut) + i * rows, rows)
+                    return full.at[pl.ds(first, rows), across]
+
+                source = shard.at[pl.ds(i * rows, rows), across]
+                cuts.append(
+                    Gather(place, source, target, rows, copies % 2 == 0, sems.at[len(cuts)])
+                )
+
+    def begin():
+        place.meet(twin=copies % 2 == 0)
+        for cut in cuts:
+            cut.start()
+
+    table = schedule(
+        (0, begin),
+        *[(2 * i + 2, cut.after_levels) for i, cut in enumerate(cuts)],
+        *[(2 * i + 4, cut.after_columns) for i, cut in enumerate(cuts[:4])],
+        *[(2 * i + 6, cut.after_twins) for i, cut in enumerate(cuts[:3])],
+    )
+    at_steps(step, table)
 
     @pl.when(pl.program_id(1) == 0)
     def _():
@@ -451,8 +739,18 @@
             mixed = part if mixed is None else mixed + part
         o_ref[rows, :] = mixed.astype(BF16)
 
-
-def attend(projected, starts, lengths):
+    @pl.when(step == steps - 1)
+    def _():
+        cuts[4].after_columns()
+        cuts[3].after_twins()
+        cuts[4].after_twins()
+        for cut in cuts:
+            cut.finish()
+        for cut in cuts:
+            cut.drain()
+
+
+def attend(projected, starts, lengths, wo, wu, wd, devices, copies):
     sequences, pieces = starts.shape
     count, columns = projected.shape
     length = count // sequences
@@ -471,37 +769,218 @@
         pl.BlockSpec((None, 2, slot, (i + 1) * slot), lambda s, p, a, b: (s, p, 0, 0))
         for i in range(pieces)
     ]
+    anywhere = pl.BlockSpec(memory_space=pl.ANY)
+    whole = [
+        jax.ShapeDtypeStruct((devices * w.shape[0], w.shape[1]), BF16) for w in (wo, wu, wd)
+    ]
     results = pl.pallas_call(
-        functools.partial(attend_kernel, slot, pieces),
-        out_shape=[jax.ShapeDtypeStruct((count, width), BF16)] + att_shapes,
+        functools.partial(attend_kernel, slot, pieces, devices, copies),
+        out_shape=[jax.ShapeDtypeStruct((count, width), BF16)] + att_shapes + whole,
         grid_spec=pltpu.PrefetchScalarGridSpec(
             num_scalar_prefetch=2,
             grid=(sequences, pairs),
-            in_specs=[part(0), part(1), part(2)],
-            out_specs=[pl.BlockSpec((length, PAIR), lambda s, p, a, b: (s, p))] + att_specs,
+            in_specs=[part(0), part(1), part(2)] + [anywhere] * 3,
+            out_specs=[pl.BlockSpec((length, PAIR), lambda s, p, a, b: (s, p))]
+            + att_specs
+            + [anywhere] * 3,
             scratch_shapes=[
                 pltpu.VMEM((length, length), F32),
                 pltpu.VMEM((1, length), F32),
+                pltpu.SemaphoreType.DMA((5, gather_sems(devices))),
             ],
         ),
-        compiler_params=params("arbitrary", "arbitrary"),
+        compiler_params=comm_params(1, "arbitrary", "arbitrary"),
         name="attend",
-    )(starts, lengths, projected, projected, projected)
-    return (results[0], results[1:])
+    )(starts, lengths, projected, projected, projected, wo, wu, wd)
+    return (results[0], results[1 : 1 + pieces], results[1 + pieces :])
 
 
 def attend_back_kernel(
-    slot, pieces, start_ref, length_ref, q_ref, k_ref, v_ref, gm_ref, o_ref, *rest
+    slot,
+    pieces,
+    chunks,
+    count,
+    copies,
+    pairs,
+    start_ref,
+    length_ref,
+    q_ref,
+    k_ref,
+    v_ref,
+    gm_ref,
+    o_ref,
+    *rest,
 ):
     att_refs = rest[:pieces]
-    gq_ref, gk_ref, gv_ref, sum_ref, later_ref, dq_ref, dk_ref, dv_ref = rest[pieces:]
-    seq, step = pl.program_id(0), pl.program_id(1)
-    last = step == pl.num_programs(1) - 1
+    rest = rest[pieces:]
+    n2_hbm, gb_hbm, hid_hbm, cot_hbm, mixed_hbm, gproj_hbm, small_ref = rest[:7]
+    gq_ref, gk_ref, gv_ref, gwo_ref, gwu_ref, gwd_ref, gsmall_ref = rest[7:14]
+    sum_ref, later_ref, dq_ref, dk_ref, dv_ref, left_ref, right_ref, load_sem = rest[14:22]
+    rest = rest[22:]
+    step = pl.program_id(0)
+    first_step = 2 * chunks + 1
+    turn = jnp.maximum(step - first_step, 0)
+    seq = lax.div(turn, pairs)
+    turn = lax.rem(turn, pairs)
+    last = turn == pairs - 1
+    width = left_ref.shape[2]
+
+    place = Place(count, copies)
+    parts = []
+    for c in range(chunks):
+
+        def write_up(value, c=c):
+            gwu_ref[:, c * width : (c + 1) * width] = value
+
+        parts.append(Scatter(place, rest[6 * c : 6 * c + 6], write_up))
+    rest = rest[6 * chunks :]
+    half_rows = gwd_ref.shape[0] // 2
+    for h in range(2):
+
+        def write_down(value, h=h):
+            gwd_ref[h * half_rows : (h + 1) * half_rows, :] = value
+
+        parts.append(Scatter(place, rest[6 * h : 6 * h + 6], write_down))
+    rest = rest[12:]
+
+    def write_out(value):
+        gwo_ref[...] = value
+
+    parts.append(Scatter(place, rest[:6], write_out))
+    small = Reduce(place, rest[6:10], gsmall_ref)
+    up_parts, (down0, down1, out_part) = (parts[:chunks], parts[chunks:])
+
+    left_slot = [0] * chunks + [(c + 1) % 2 for c in range(chunks)] + [(chunks + 1) % 2]
+    right_slot = [c % 2 for c in range(chunks)] + [chunks % 2] * chunks + [(chunks + 1) % 2]
+
+    def chunk_of(ref, c):
+        return ref.at[:, pl.ds(c * width, width)]
+
+    left_loads = {0: n2_hbm, 2 * chunks: mixed_hbm}
+    right_loads = {chunks: cot_hbm, 2 * chunks: gproj_hbm}
+    for c in range(chunks):
+        left_loads[chunks + c] = chunk_of(hid_hbm, c)
+        right_loads[c] = chunk_of(gb_hbm, c)
+
+    def loads(when):
+        copies = []
+        if when in left_loads:
+            at = left_slot[when]
+            copies.append(
+                pltpu.make_async_copy(left_loads[when], left_ref.at[at], load_sem.at[at])
+            )
+        if when in right_loads:
+            at = right_slot[when]
+            copies.append(
+                pltpu.make_async_copy(right_loads[when], right_ref.at[at], load_sem.at[2 + at])
+            )
+        return copies
+
+    def begin():
+        for copy in loads(0):
+            copy.start()
+        place.meet(copies=True)
+        small.start(small_ref[...])
+
+    entries = [(0, begin)]
+    for c, part in enumerate(up_parts):
+        entries += [
+            (c + 2, part.after_cores),
+            (2 * c + 5, part.after_columns),
+            (2 * c + 8, part.after_levels),
+            (2 * c + 10, part.after_copies),
+        ]
+    entries += [
+        (3, small.after_cores),
+        (6, small.after_columns),
+        (10, small.after_levels),
+        (13, small.after_copies),
+        (first_step, down0.after_cores),
+        (first_step + 1, down1.after_cores),
+        (first_step + 1, out_part.after_cores),
+        (first_step + 4, down0.after_columns),
+        (first_step + 6, down1.after_columns),
+        (first_step + 7, out_part.after_columns),
+        (first_step + 7, down0.after_levels),
+        (first_step + 9, down0.after_copies),
+        (first_step + 9, down1.after_levels),
+        (first_step + 10, out_part.after_levels),
+        (first_step + 11, down1.after_copies),
+    ]
+    at_steps(step, schedule(*entries))
+
+    @pl.when(step < first_step)
+    def _():
+        left_at = jnp.zeros((), jnp.int32)
+        right_at = jnp.zeros((), jnp.int32)
+        for when in range(first_step):
+
+            @pl.when(step == when)
+            def _(when=when):
+                if when + 1 < first_step:
+                    for copy in loads(when + 1):
+                        copy.start()
+                for copy in loads(when):
+                    copy.wait()
+
+            left_at = jnp.where(step == when, left_slot[when], left_at)
+            right_at = jnp.where(step == when, right_slot[when], right_at)
+        grad = dot_tn(left_ref[left_at], right_ref[right_at]).astype(BF16)
+        for when in range(first_step):
+
+            @pl.when(step == when)
+            def _(when=when):
+                if when < chunks or when == 2 * chunks:
+                    part = out_part if when == 2 * chunks else up_parts[when]
+                    rows = width // count
+                    for block in range(count):
+                        part.held[block] = grad[block * rows : (block + 1) * rows, :]
+                    part.start()
+                else:
+                    blocks = count // chunks
+                    for i in range(blocks):
+                        block = (when - chunks) * blocks + i
+                        for h, part in enumerate((down0, down1)):
+                            at = (2 * i + h) * half_rows
+                            part.held[block] = grad[at : at + half_rows, :]
+                    if when == 2 * chunks - 1:
+                        down0.start()
+                        down1.start()
+
+    @pl.when(step >= first_step)
+    def _():
+        attend_back_step(
+            slot,
+            pieces,
+            seq,
+            turn,
+            last,
+            start_ref,
+            length_ref,
+            (q_ref, k_ref, v_ref, gm_ref, o_ref),
+            att_refs,
+            (gq_ref, gk_ref, gv_ref),
+            (sum_ref, later_ref, dq_ref, dk_ref, dv_ref),
+        )
+
+    @pl.when(step == pl.num_programs(0) - 1)
+    def _():
+        out_part.after_copies()
+        for part in parts + [small]:
+            part.drain()
+
+
+def attend_back_step(
+    slot, pieces, seq, turn, last, start_ref, length_ref, inputs, att_refs, outs, scratch
+):
+    q_ref, k_ref, v_ref, gm_ref, o_ref = inputs
+    gq_ref, gk_ref, gv_ref = outs
+    sum_ref, later_ref, dq_ref, dk_ref, dv_ref = scratch
     length = q_ref.shape[0]
     zero = jnp.zeros((), BF16)
     scale = jnp.asarray(SCALE, BF16)
 
-    @pl.when(step == 0)
+    @pl.when(turn == 0)
     def _():
         sum_ref[...] = jnp.zeros_like(sum_ref)
 
@@ -561,44 +1040,92 @@
     gv_ref[...] = dv_ref[...].astype(BF16)
 
 
-def attend_back(projected, starts, lengths, grad_mixed, mixed, attention):
+def attend_back(
+    projected, starts, lengths, grad_mixed, mixed, attention, kept, small, devices, copies
+):
+    n2, grad_before, hidden, cotangent, grad_proj = kept
     sequences, pieces = starts.shape
     count, columns = projected.shape
     length = count // sequences
     slot = length // pieces
     width = columns // 3
     pairs = width // PAIR
+    chunks = hidden.shape[1] // width
+    first_step = 2 * chunks + 1
+    rows = width // devices
+    down_rows = hidden.shape[1] // devices
+    lines = small.shape[0]
+
+    def turn(step):
+        at = jnp.maximum(step - first_step, 0)
+        return (lax.div(at, pairs), pairs - 1 - lax.rem(at, pairs))
 
     def part(which):
-        return pl.BlockSpec(
-            (length, PAIR), lambda s, p, a, b: (s, which * pairs + pairs - 1 - p)
-        )
-
-    att_specs = [
-        pl.BlockSpec(
-            (None, 2, slot, (i + 1) * slot), lambda s, p, a, b: (s, pairs - 1 - p, 0, 0)
-        )
-        for i in range(pieces)
+        def index(step, a, b):
+            seq, pair = turn(step)
+            return (seq, which * pairs + pair)
+
+        return pl.BlockSpec((length, PAIR), index)
+
+    def att_index(step, a, b):
+        seq, pair = turn(step)
+        return (seq, pair, 0, 0)
+
+    att_specs = [pl.BlockSpec((None, 2, slot, (i + 1) * slot), att_index) for i in range(pieces)]
+    anywhere = pl.BlockSpec(memory_space=pl.ANY)
+
+    def fixed(shape):
+        return pl.BlockSpec(shape, lambda *_: (0,) * len(shape))
+
+    results = [(rows, width), (rows, chunks * width), (down_rows, width), (lines, 1, width)]
+    scratch = [
+        pltpu.VMEM((length, length), F32),
+        pltpu.VMEM((1, length), F32),
+        pltpu.VMEM((length, PAIR), F32),
+        pltpu.VMEM((length, PAIR), F32),
+        pltpu.VMEM((length, PAIR), F32),
+        pltpu.VMEM((2, count, width), BF16),
+        pltpu.VMEM((2, count, width), BF16),
+        pltpu.SemaphoreType.DMA((4,)),
     ]
+    for piece_rows in [rows] * chunks + [down_rows // 2] * 2 + [rows]:
+        scratch += scatter_scratch(devices, copies, piece_rows, width)
+    scratch += reduce_scratch(devices, copies, lines, width)
     return pl.pallas_call(
-        functools.partial(attend_back_kernel, slot, pieces),
-        out_shape=[jax.ShapeDtypeStruct((count, width), BF16)] * 3,
+        functools.partial(
+            attend_back_kernel, slot, pieces, chunks, devices, copies, pairs
+        ),
+        out_shape=[jax.ShapeDtypeStruct((count, width), BF16)] * 3
+        + [jax.ShapeDtypeStruct(shape, F32) for shape in results],
         grid_spec=pltpu.PrefetchScalarGridSpec(
             num_scalar_prefetch=2,
-            grid=(sequences, pairs),
-            in_specs=[part(0), part(1), part(2), part(0), part(0)] + att_specs,
-            out_specs=[part(0), part(0), part(0)],
-            scratch_shapes=[
-                pltpu.VMEM((length, length), F32),
-                pltpu.VMEM((1, length), F32),
-                pltpu.VMEM((length, PAIR), F32),
-                pltpu.VMEM((length, PAIR), F32),
-                pltpu.VMEM((length, PAIR), F32),
-            ],
+            grid=(first_step + sequences * pairs,),
+            in_specs=[part(0), part(1), part(2), part(0), part(0)]
+            + att_specs
+            + [anywhere] * 6
+            + [fixed((lines, 1, width))],
+            out_specs=[part(0), part(0), part(0)] + [fixed(shape) for shape in results],
+            scratch_shapes=scratch,
         ),
-        compiler_params=params("arbitrary", "arbitrary"),
+        compiler_params=comm_params(2, "arbitrary"),
         name="attend_back",
-    )(starts, lengths, projected, projected, projected, grad_mixed, mixed, *attention)
+    )(
+        starts,
+        lengths,
+        projected,
+        projected,
+        projected,
+        grad_mixed,
+        mixed,
+        *attention,
+        n2,
+        grad_before,
+        hidden,
+        cotangent,
+        mixed,
+        grad_proj,
+        small,
+    )
 
 
 def gelu_and_slope(values):
@@ -628,39 +1155,32 @@
     gmid_ref,
     gmix_ref,
     small_ref,
-    gwo_hbm,
-    gwu_hbm,
-    gwd_hbm,
+    n2_ref,
+    hid_ref,
+    gb_ref,
+    gproj_ref,
     wo_ref,
     wu_ref,
     wd_ref,
-    gwo_ref,
-    gwu_ref,
-    gwd_ref,
     acc_ref,
     gnorm_ref,
-    n2_ref,
     mid_ref,
-    stage_ref,
     load_sem,
-    stage_sem,
 ):
     step = pl.program_id(0)
-    steps = pl.num_programs(0)
     chunks = wu_ref.shape[0]
-    width = x_ref.shape[1]
 
     def load_out():
         return pltpu.make_async_copy(wo_hbm, wo_ref, load_sem.at[0])
 
     def load_up(c):
         return pltpu.make_async_copy(
-            wu_hbm.at[:, pl.ds(c * chunk, chunk)], wu_ref.at[c], load_sem.at[1]
+            wu_hbm.at[:, pl.ds(c * chunk, chunk)], wu_ref.at[c], load_sem.at[1 + 2 * c]
         )
 
     def load_down(c):
         return pltpu.make_async_copy(
-            wd_hbm.at[pl.ds(c * chunk, chunk), :], wd_ref.at[c], load_sem.at[2]
+            wd_hbm.at[pl.ds(c * chunk, chunk), :], wd_ref.at[c], load_sem.at[2 + 2 * c]
         )
 
     @pl.when(step == 0)
@@ -668,11 +1188,7 @@
         load_out().start()
         for c in range(chunks):
             load_up(c).start()
-        for c in range(chunks):
             load_down(c).start()
-        gwo_ref[...] = jnp.zeros_like(gwo_ref)
-        gwu_ref[...] = jnp.zeros_like(gwu_ref)
-        gwd_ref[...] = jnp.zeros_like(gwd_ref)
         small_ref[...] = jnp.zeros_like(small_ref)
         load_out().wait()
 
@@ -682,7 +1198,6 @@
     def _():
         for c in range(chunks):
             load_up(c).wait()
-        for c in range(chunks):
             load_down(c).wait()
 
     normed, _ = normalize(mid_ref[...])
@@ -691,16 +1206,17 @@
     gnorm_ref[...] = jnp.zeros_like(gnorm_ref)
 
     def one_chunk(c, carry):
+        columns = pl.ds(pl.multiple_of(c * chunk, chunk), chunk)
         before = dot(n2_ref[...], wu_ref[c]) + up_bias_ref[c]
         hidden, slope = gelu_and_slope(before)
         hidden = hidden.astype(BF16)
+        hid_ref[:, columns] = hidden
         acc_ref[...] += dot(hidden, wd_ref[c])
-        gwd_ref[c] += dot_tn(hidden, cot_ref[...])
         grad_hidden = dot_nt(cot_ref[...], wd_ref[c]).astype(BF16)
         grad_before = (grad_hidden.astype(F32) * slope).astype(BF16)
+        gb_ref[:, columns] = grad_before
         small_ref[3 + c] += column_sum(grad_before.astype(F32))
         gnorm_ref[...] += dot_nt(grad_before, wu_ref[c])
-        gwu_ref[c] += dot_tn(n2_ref[...], grad_before)
         return carry
 
     lax.fori_loop(0, chunks, one_chunk, 0)
@@ -715,28 +1231,8 @@
     grad_middle = cot + norm_back(grad_normed * gain_ref[...], normed, inverse)
     gmid_ref[...] = grad_middle
     grad_proj = grad_middle.astype(BF16)
-    gwo_ref[...] += dot_tn(mixed_ref[...], grad_proj)
+    gproj_ref[...] = grad_proj
     gmix_ref[...] = dot_nt(grad_proj, wo_ref[...]).astype(BF16)
-
-    @pl.when(step == steps - 1)
-    def _():
-        copies = []
-
-        def put(value, target):
-            i = len(copies)
-            if i >= 2:
-                copies[i - 2].wait()
-            stage_ref[i % 2] = value.astype(BF16)
-            copy = pltpu.make_async_copy(stage_ref.at[i % 2], target, stage_sem.at[i % 2])
-            copy.start()
-            copies.append(copy)
-
-        put(gwo_ref[...], gwo_hbm)
-        for c in range(chunks):
-            put(gwu_ref[c], gwu_hbm.at[:, pl.ds(c * chunk, chunk)])
-            put(gwd_ref[c], gwd_hbm.at[pl.ds(c * chunk, chunk), :])
-        copies[-2].wait()
-        copies[-1].wait()
 
 
 def vector_line(row):
@@ -751,16 +1247,22 @@
     chunks = hidden // chunk
     rows = pl.BlockSpec((block, width), lambda i: (i, 0))
     anywhere = pl.BlockSpec(memory_space=pl.ANY)
+    wide = pl.BlockSpec((block, hidden), lambda i: (i, 0))
+
+    def low(columns):
+        return jax.ShapeDtypeStruct((count, columns), BF16)
+
     return pl.pallas_call(
         functools.partial(feed_kernel, chunk),
         out_shape=[
-            jax.ShapeDtypeStruct((count, width), BF16),
+            low(width),
             jax.ShapeDtypeStruct((count, width), F32),
-            jax.ShapeDtypeStruct((count, width), BF16),
+            low(width),
             jax.ShapeDtypeStruct((3 + chunks, 1, width), F32),
-            jax.ShapeDtypeStruct(wo.shape, BF16),
-            jax.ShapeDtypeStruct(wu.shape, BF16),
-            jax.ShapeDtypeStruct(wd.shape, BF16),
+            low(width),
+            low(hidden),
+            low(hidden),
+            low(width),
         ],
         grid=(count // block,),
         in_specs=[
@@ -780,24 +1282,19 @@
             rows,
             rows,
             pl.BlockSpec((3 + chunks, 1, width), lambda i: (0, 0, 0)),
-            anywhere,
-            anywhere,
-            anywhere,
+            rows,
+            wide,
+            wide,
+            rows,
         ],
         scratch_shapes=[
             pltpu.VMEM(wo.shape, BF16),
             pltpu.VMEM((chunks, width, chunk), BF16),
             pltpu.VMEM((chunks, chunk, width), BF16),
-            pltpu.VMEM(wo.shape, F32),
-            pltpu.VMEM((chunks, width, chunk), F32),
-            pltpu.VMEM((chunks, chunk, width), F32),
             pltpu.VMEM((block, width), F32),
             pltpu.VMEM((block, width), F32),
-            pltpu.VMEM((block, width), BF16),
             pltpu.VMEM((block, width), F32),
-            pltpu.VMEM((2, width, chunk), BF16),
-            pltpu.SemaphoreType.DMA((3,)),
-            pltpu.SemaphoreType.DMA((2,)),
+            pltpu.SemaphoreType.DMA((1 + 2 * chunks,)),
         ],
         compiler_params=params("arbitrary"),
         name="feed",
@@ -816,73 +1313,165 @@
 
 
 def input_kernel(
-    x_ref,
+    count,
+    copies,
     gmid_ref,
-    gq_ref,
-    gk_ref,
-    gv_ref,
     gain_ref,
     shift_ref,
+    x_hbm,
+    gq_hbm,
+    gk_hbm,
+    gv_hbm,
+    w_hbm,
+    gx_ref,
+    gw_ref,
+    gsmall_ref,
+    x_ref,
+    n1_ref,
+    g_ref,
     w_ref,
-    gx_ref,
     small_ref,
-    gw_ref,
-    acc_ref,
+    load_sem,
+    *rest,
 ):
     step = pl.program_id(0)
-    width = x_ref.shape[1]
-
-    @pl.when(step == 0)
-    def _():
-        acc_ref[...] = jnp.zeros_like(acc_ref)
+    total, width = x_ref.shape
+    block = gx_ref.shape[0]
+    place = Place(count, copies)
+    parts = []
+    for which in range(3):
+
+        def write(value, which=which):
+            gw_ref[:, which * width : (which + 1) * width] = value
+
+        parts.append(Scatter(place, rest[6 * which : 6 * which + 6], write))
+    small = Reduce(place, rest[18:22], gsmall_ref)
+
+    def load_x():
+        return pltpu.make_async_copy(x_hbm, x_ref, load_sem.at[0])
+
+    def load_grad(which):
+        source = (gq_hbm, gk_hbm, gv_hbm)[which]
+        return pltpu.make_async_copy(source, g_ref.at[which], load_sem.at[1 + which])
+
+    def load_weight():
+        return pltpu.make_async_copy(w_hbm, w_ref, load_sem.at[4])
+
+    def begin():
+        load_x().start()
+        for which in range(3):
+            load_grad(which).start()
+        load_weight().start()
+        place.meet(copies=True)
         small_ref[...] = jnp.zeros_like(small_ref)
-
-    normed, inverse = normalize(x_ref[...].astype(F32))
-    low = (normed * gain_ref[...] + shift_ref[...]).astype(BF16)
-    grad_normed = None
-    for which, ref in enumerate((gq_ref, gk_ref, gv_ref)):
-        grad = ref[...]
-        acc_ref[which] += dot_tn(low, grad)
-        part = dot_nt(grad, w_ref[:, which * width : (which + 1) * width])
-        grad_normed = part if grad_normed is None else grad_normed + part
-    small_ref[0] += column_sum(grad_normed * normed)
-    small_ref[1] += column_sum(grad_normed)
-    gx_ref[...] = gmid_ref[...] + norm_back(grad_normed * gain_ref[...], normed, inverse)
+        load_x().wait()
+
+        def norm_rows(i, carry):
+            at = pl.ds(pl.multiple_of(i * 256, 256), 256)
+            normed, _ = normalize(x_ref[at, :].astype(F32))
+            n1_ref[at, :] = (normed * gain_ref[...] + shift_ref[...]).astype(BF16)
+            return carry
+
+        lax.fori_loop(0, total // 256, norm_rows, 0)
+
+    table = schedule(
+        (0, begin),
+        (1, parts[0].after_cores),
+        (2, parts[1].after_cores),
+        (3, parts[2].after_cores),
+        (4, parts[0].after_columns),
+        (5, parts[1].after_columns),
+        (6, parts[2].after_columns),
+        (6, parts[0].after_levels),
+    )
+    at_steps(step, table)
+
+    @pl.when(step < 3)
+    def _():
+        for which in range(3):
+
+            @pl.when(step == which)
+            def _(which=which):
+                load_grad(which).wait()
+
+        grad = dot_tn(n1_ref[...], g_ref[step]).astype(BF16)
+        for which in range(3):
+
+            @pl.when(step == which)
+            def _(which=which):
+                rows = width // count
+                for i in range(count):
+                    parts[which].held[i] = grad[i * rows : (i + 1) * rows, :]
+                parts[which].start()
+
+    @pl.when(step == 3)
+    def _():
+        load_weight().wait()
+
+    @pl.when(step >= 3)
+    def _():
+        at = pl.ds(pl.multiple_of((step - 3) * block, block), block)
+        normed, inverse = normalize(x_ref[at, :].astype(F32))
+        grad_normed = None
+        for which in range(3):
+            part = dot_nt(g_ref[which, at, :], w_ref[:, which * width : (which + 1) * width])
+            grad_normed = part if grad_normed is None else grad_normed + part
+        small_ref[0] += column_sum(grad_normed * normed)
+        small_ref[1] += column_sum(grad_normed)
+        gx_ref[...] = gmid_ref[...] + norm_back(grad_normed * gain_ref[...], normed, inverse)
 
     @pl.when(step == pl.num_programs(0) - 1)
     def _():
-        for which in range(3):
-            gw_ref[:, which * width : (which + 1) * width] = acc_ref[which].astype(BF16)
-
-
-def input_back(tokens, grad_middle, grads, vectors, weight):
+        small.start(small_ref[...])
+        parts[1].after_levels()
+        small.after_cores()
+        parts[0].after_copies()
+        small.after_columns()
+        parts[2].after_levels()
+        parts[1].after_copies()
+        small.after_levels()
+        parts[2].after_copies()
+        small.after_copies()
+        for part in parts + [small]:
+            part.drain()
+
+
+def input_back(tokens, grad_middle, grads, vectors, weight, devices, copies):
     count, width = tokens.shape
     block = 512
-    rows = pl.BlockSpec((block, width), lambda i: (i, 0))
+    shard = width // devices
+    rows = pl.BlockSpec((block, width), lambda i: (jnp.maximum(i - 3, 0), 0))
+    anywhere = pl.BlockSpec(memory_space=pl.ANY)
+    scratch = [
+        pltpu.VMEM((count, width), BF16),
+        pltpu.VMEM((count, width), BF16),
+        pltpu.VMEM((3, count, width), BF16),
+        pltpu.VMEM(weight.shape, BF16),
+        pltpu.VMEM((2, 1, width), F32),
+        pltpu.SemaphoreType.DMA((5,)),
+    ]
+    for _ in range(3):
+        scratch += scatter_scratch(devices, copies, shard, width)
+    scratch += reduce_scratch(devices, copies, 2, width)
     return pl.pallas_call(
-        input_kernel,
+        functools.partial(input_kernel, devices, copies),
         out_shape=[
             jax.ShapeDtypeStruct((count, width), F32),
+            jax.ShapeDtypeStruct((shard, 3 * width), F32),
             jax.ShapeDtypeStruct((2, 1, width), F32),
-            jax.ShapeDtypeStruct(weight.shape, BF16),
         ],
-        grid=(count // block,),
-        in_specs=[rows] * 5
-        + [vector_line(GAIN1)(width), vector_line(SHIFT1)(width)]
-        + [pl.BlockSpec(weight.shape, lambda i: (0, 0))],
+        grid=(3 + count // block,),
+        in_specs=[rows, vector_line(GAIN1)(width), vector_line(SHIFT1)(width)]
+        + [anywhere] * 5,
         out_specs=[
             rows,
+            pl.BlockSpec((shard, 3 * width), lambda i: (0, 0)),
             pl.BlockSpec((2, 1, width), lambda i: (0, 0, 0)),
-            pl.BlockSpec(weight.shape, lambda i: (0, 0)),
         ],
-        scratch_shapes=[pltpu.VMEM((3, width, width), F32)],
-        compiler_params=params("arbitrary"),
+        scratch_shapes=scratch,
+        compiler_params=comm_params(3, "arbitrary"),
         name="input_back",
-    )(tokens, grad_middle, *grads, vectors, vectors, weight)
-
-
-def gather(value):
-    return lax.all_gather(value, "fsdp", axis=0, tiled=True)
+    )(grad_middle, vectors, vectors, tokens, *grads, weight)
 
 
 def local(
@@ -914,52 +1503,54 @@
     own = jnp.concatenate([placed(vector) for vector in own], axis=0)
     own = jnp.pad(own, ((0, LINES - own.shape[0]), (0, 0)))
 
-    wo = gather(output_weight)
-    wu = gather(up_weight)
-    wd = gather(down_weight)
-
     projected, wqkv, vectors = project(tokens, query_key_value, own, devices, copies)
-    mixed, attention = attend(projected, piece_start, piece_length)
-    block_output, grad_middle, grad_mixed, small2, gwo, gwu, gwd = feed(
+    mixed, attention, (wo, wu, wd) = attend(
+        projected,
+        piece_start,
+        piece_length,
+        output_weight,
+        up_weight,
+        down_weight,
+        devices,
+        copies,
+    )
+    block_output, grad_middle, grad_mixed, small2, n2, hidden, grad_before, grad_proj = feed(
         tokens, mixed, cotangent, vectors, wo, wu, wd
     )
-    grads = attend_back(projected, piece_start, piece_length, grad_mixed, mixed, attention)
-    grad_tokens, small1, gwqkv = input_back(tokens, grad_middle, grads, vectors, wqkv)
-
-    small = jnp.concatenate([small1.reshape(-1, width), small2.reshape(-1, width)], axis=0)
-
-    def scatter(value):
-        return lax.psum_scatter(value, "fsdp", scatter_dimension=0, tiled=True)
-
-    def across(value):
-        return lax.psum(value, "rep").astype(F32)
-
-    small = small.astype(BF16)
-    order = [small[0], small[1], small[2], small[3], small[5:].reshape(-1), small[4]]
-    sizes = [v.size // devices for v in order]
-    total = sum(sizes)
-    padded = -(-total // 1024) * 1024
-    packed = jnp.concatenate([v.reshape(devices, -1) for v in order], axis=1)
-    packed = jnp.pad(packed, ((0, 0), (0, padded - total))).reshape(devices * 8, padded // 8)
-    packed = across(scatter(packed)).reshape(-1)
-    tails, at = ([], 0)
-    for size in sizes:
-        tails.append(packed[at : at + size])
-        at += size
-    gfg, gfs, gsg, gss, gub, gdb = tails
+    *grads, gwo, gwu, gwd, small2 = attend_back(
+        projected,
+        piece_start,
+        piece_length,
+        grad_mixed,
+        mixed,
+        attention,
+        (n2, grad_before, hidden, cotangent, grad_proj),
+        small2,
+        devices,
+        copies,
+    )
+    grad_tokens, gwqkv, small1 = input_back(
+        tokens, grad_middle, grads, vectors, wqkv, devices, copies
+    )
+
+    def mine(values):
+        values = values.reshape(-1)
+        size = values.shape[0] // devices
+        return lax.dynamic_slice(values, (index * size,), (size,))
+
     return (
         block_output,
         grad_tokens,
-        across(scatter(gwqkv)),
-        across(scatter(gwo)),
-        across(scatter(gwu)),
-        across(scatter(gwd)),
-        gfg,
-        gfs,
-        gsg,
-        gss,
-        gub,
-        gdb,
+        gwqkv,
+        gwo,
+        gwu,
+        gwd,
+        mine(small1[0]),
+        mine(small1[1]),
+        mine(small2[0]),
+        mine(small2[1]),
+        mine(small2[3:]),
+        mine(small2[2]),
     )
 
 

time: 670 us -> 399 us (0.60)
  waiting for transfers between devices: 260 us -> 0 us
  Pallas kernels: 309 us -> 377 us
  blocking collectives: 63 us -> 0 us
  between operations: 15.2 us -> 1.03 us
  local copies, waits for them, and re-layouts: 8.09 us -> 17.7 us
  other arithmetic: 6.93 us -> 0 us
    reduce_scatter x4 -> x0, waiting for transfers between devices: 222 us -> none  [scatter(): return lax.psum_scatter(value, 'fsdp', scatter_dimension=0, tiled=True)]
    pallas_call x4, Pallas kernels: 251 us -> 324 us  [the longest x1 121 us: attend_back(): pl.pallas_call(functools.partial(attend_back_kernel, slot, pieces, chunks...]
    unnamed x1 -> x0, blocking collectives: 58 us -> none
    all_gather x3 -> x0, waiting for transfers between devices: 34.1 us -> none  [gather(): return lax.all_gather(value, 'fsdp', axis=0, tiled=True)]
    unnamed x7 -> x15, local copies, waits for them, and re-layouts: 0.6 us -> 9.09 us
    convert_element_type x4 -> x0, other arithmetic: 6.91 us -> none  [across(): return lax.psum(value, 'rep').astype(F32)]
  transfers between devices with their start and end apart: 8 -> 0, of which waited for: 4 -> 0; matrix products, arithmetic and copies ran while one was open for 1% -> 0% of each run, Pallas kernels for 31% -> 0%
where the time goes in v3:
time: 399 us; the launch traced here: 396 us
  Pallas kernels  377 us (94%)
  local copies, waits for them, and re-layouts  17.7 us (4%)
    pallas_call x1, Pallas kernels, attend_back(): pl.pallas_call(functools.partial(attend_back_kernel, slot, pieces, chunks...  121 us
    pallas_call x1, Pallas kernels, attend(): pl.pallas_call(functools.partial(attend_kernel, slot, pieces, devices, co...  76.4 us
    pallas_call x1, Pallas kernels, feed(): pl.pallas_call(functools.partial(feed_kernel, chunk), out_shape=[low(widt...  73.3 us
    pallas_call x1, Pallas kernels, project(): pl.pallas_call(functools.partial(project_kernel, count, copies), out_shap...  53.1 us
    pallas_call x1, Pallas kernels, input_back(): pl.pallas_call(functools.partial(input_kernel, devices, copies), out_shap...  52.7 us
    unnamed x15, local copies, waits for them, and re-layouts  9.09 us

profile of v3, /device:TPU:0, one launch (start us, length us, event | category | flops | bytes accessed | tf_op | source)
XLA Modules:
  0.0 395.6 jit_solution(7463631430822580799)
XLA Ops:
  0.7 0.8 dynamic_update_slice.27
  1.5 0.8 dynamic_update_slice.26
  2.3 0.8 dynamic_update_slice.25
  3.1 0.8 dynamic_update_slice.24
  3.9 0.8 dynamic_update_slice.28
  4.7 0.9 dynamic_update_slice.23
  5.6 0.1 concatenate.3
  5.6 0.6 pad.4.vec_hbm
  6.2 53.1 %project.1 = (bf16[2048,2304]{1,0:T(8,128)(2,1)}, bf16[768,2304]{1,0:T(8,128)(2,1)}, f32[16,1,768]{2,1,0:T(1,128)}) custom-call(bf16[2048,768]{1,0:T(8,128)(2,1)} %x_hbm.1, bf16[48,2304]{1,0:T(8,128)(2,1)} %w_hbm.1, bf16[16,768]{1,0:T(8,128)(2,1)} %pad.4.vec_hbm), custom_call_target="tpu_custom_call" | custom-call | tf_op jit(solution)/shard_map/project/pallas_call | solution.py:570
  59.4 76.4 %attend.1 = (bf16[2048,768]{1,0:T(8,128)(2,1)}, bf16[2,12,512,512]{3,2,1,0:T(8,128)(2,1)}, bf16[2,12,512,1024]{3,2,1,0:T(8,128)(2,1)}, bf16[768,768]{1,0:T(8,128...) custom-call(s32[2,2]{1,0:T(2,128)} %start_ref.3, s32[2,2]{1,0:T(2,128)} %length_ref.3, ...), custom_call_target="tpu_custom_call" | custom-call | tf_op jit(solution)/shard_map/attend/pallas_call | solution.py:776
  135.8 73.3 %feed.1 = (bf16[2048,768]{1,0:T(8,128)(2,1)}, f32[2048,768]{1,0:T(8,128)}, bf16[2048,768]{1,0:T(8,128)(2,1)}, f32[7,1,768]{2,1,0:T(1,128)}, bf16[2048,768]{1,0:T...) custom-call(bf16[2048,768]{1,0:T(8,128)(2,1)} %x_hbm.1, ...), custom_call_target="tpu_custom_call" | custom-call | tf_op jit(solution)/shard_map/feed/pallas_call | solution.py:1255
  209.1 121.4 %attend_back.1 = (bf16[2048,768]{1,0:T(8,128)(2,1)}, bf16[2048,768]{1,0:T(8,128)(2,1)}, bf16[2048,768]{1,0:T(8,128)(2,1)}, f32[48,768]{1,0:T(8,128)}, f32[48,307...) custom-call(s32[2,2]{1,0:T(2,128)} %start_ref.3, s32[2,2]{1,0:T(2,128)} %length_ref.3, ...), custom_call_target="tpu_custom_call" | custom-call | tf_op jit(solution)/shard_map/attend_back/pallas_call | solution.py:1094
  330.5 0.0 copy-start.4
  330.5 52.7 %input_back.1 = (f32[2048,768]{1,0:T(8,128)}, f32[48,2304]{1,0:T(8,128)}, f32[2,1,768]{2,1,0:T(1,128)}) custom-call(f32[2048,768]{1,0:T(8,128)} %get-tuple-element.46.gmid_ref, f32[16,1,768]{2,1,0:T(1,128)} %get-tuple-element.41.gain_ref.shift_ref.up_bias_ref.down_bias_ref, f32[16,1,768]{2,1,0:T(1,128)} %get-tuple-element.41.gain_ref.shift_ref.up_bias_ref.down_bias_ref, ...), custom_call_target="tpu_custom_call" | custom-call | tf_op jit(solution)/shard_map/input_back/pallas_call | solution.py:1456
  383.2 0.7 fusion.6
  383.9 0.6 fusion
  384.5 0.0 copy-done.4
  384.5 0.6 dynamic_slice.36
  385.1 0.6 fusion.4
  385.7 0.6 fusion.2
  386.3 0.0 copy-start.2
  386.3 0.0 copy-start.3
  386.3 0.0 copy-start.1
  386.3 0.0 copy-start
  386.3 6.0 %copy.38 = f32[2048,768]{1,0:T(8,128)} copy(f32[2048,768]{1,0:T(8,128)} %get-tuple-element.88) | data formatting | bytes 12582912
  392.3 0.0 copy-done.2
  392.3 0.8 copy.39
  393.1 0.0 copy-done.3
  393.1 0.7 copy.40
  393.7 0.0 copy-done.1
  393.8 0.8 copy.41
  394.6 0.0 copy-done
  394.6 0.8 copy.42
  (9 shorter events, 0.0 us)
Async XLA Ops:
  330.5 54.0 %copy-start.4 = (f32[7,1,768]{2,1,0:T(1,128)S(1)}, f32[7,1,768]{2,1,0:T(1,128)}, u32[]{:S(2)}) copy-start(f32[7,1,768]{2,1,0:T(1,128)} %get-tuple-element.65) | copy-start | bytes 64516
  386.3 6.0 %copy-start.2 = (f32[48,2304]{1,0:T(8,128)S(1)}, f32[48,2304]{1,0:T(8,128)}, u32[]{:S(2)}) copy-start(f32[48,2304]{1,0:T(8,128)} %get-tuple-element.89) | copy-start | bytes 1327108
  386.3 6.8 %copy-start.3 = (f32[48,768]{1,0:T(8,128)S(1)}, f32[48,768]{1,0:T(8,128)}, u32[]{:S(2)}) copy-start(f32[48,768]{1,0:T(8,128)} %get-tuple-element.90) | copy-start | bytes 442372
  386.3 7.5 %copy-start.1 = (f32[48,3072]{1,0:T(8,128)S(1)}, f32[48,3072]{1,0:T(8,128)}, u32[]{:S(2)}) copy-start(f32[48,3072]{1,0:T(8,128)} %get-tuple-element.91) | copy-start | bytes 1769476
  386.3 8.3 %copy-start = (f32[192,768]{1,0:T(8,128)S(1)}, f32[192,768]{1,0:T(8,128)}, u32[]{:S(2)}) copy-start(f32[192,768]{1,0:T(8,128)} %get-tuple-element.92) | copy-start | bytes 1769476
